TPU v7x, 32 devices: a whole 2x2x4 slice. The times are simulated.
32 devices in a mesh: seq: 8 (over z, x), dp: 4 (over y, core).
Axes of the slice: x: 2, y: 2, z: 4, core: 2. Of those that a mesh axis runs over, the one named last changes fastest.
Arguments:
- layer_input: bfloat16 [4, 1024, 4096], P('dp', 'seq'), may hold values from -6 to 6
- projection: bfloat16 [4096, 256], replicated, may hold values from -0.09375 to 0.09375
- ssm_input: bfloat16 [4, 1024, 4096], P('dp', 'seq'), may hold values from -6 to 6
- step_logit: float32 [4, 1024, 64], P('dp', 'seq'), may hold values from -4 to 4
- decay_rate: float32 [64], replicated, may hold values from 0.00048828125 to 0.1
- output_grad: bfloat16 [4, 1024, 4096], P('dp', 'seq'), may hold values from -6 to 6
Outputs:
- input_grad: bfloat16 [4, 1024, 4096], P('dp', 'seq')
- step_grad: float32 [4, 1024, 64], P('dp', 'seq')
- rate_grad: float32 [64], replicated
- projection_grad: float32 [4096, 256], P('seq')
All inputs are finite; a program needn't handle non-finite values.
Results may differ from a plain program's by a relative error of at most 0.011.
Values sent between devices are 32-bit elements; how exact they have to be, the bound alone decides.
A program may use at most 320 MiB of HBM per device.

v0:
```python
import jax
import jax.numpy as jnp
from jax import lax
from jax.sharding import PartitionSpec as P


def carried_in(value, axis, join, neutral, backward):
    count, mine = (lax.axis_size(axis), lax.axis_index(axis))
    pieces = jax.tree.map(lambda part: lax.all_gather(part, axis), value)
    if backward:
        pieces = jax.tree.map(lambda part: part[::-1], pieces)
        mine = count - 1 - mine
    subtotal = jax.tree.map(
        lambda part, zero: jnp.full_like(part, 0) + jnp.asarray(zero, part.dtype), value, neutral
    )

    def lap(position, subtotal):
        longer = join(subtotal, jax.tree.map(lambda part: part[position], pieces))
        return jax.tree.map(lambda new, old: jnp.where(position < mine, new, old), longer, subtotal)

    return lax.fori_loop(0, count - 1, lap, subtotal)


def span_forward(ssm_block, b_block, c_block, logit_block, decay_rate, carry_in):
    row_count = ssm_block.shape[0]
    head_count = logit_block.shape[1]
    values = ssm_block.astype(jnp.float32).reshape(row_count, head_count, -1)
    b_vals = b_block.astype(jnp.float32)
    c_vals = c_block.astype(jnp.float32)
    dt_soft = jax.nn.softplus(logit_block)
    log_decay = jnp.cumsum(-decay_rate[None, :] * dt_soft, axis=0)
    causal = (
        lax.broadcasted_iota(jnp.int32, (row_count, row_count), 0)
        >= lax.broadcasted_iota(jnp.int32, (row_count, row_count), 1)
    )[None, :, :]
    decay_heads = log_decay.T
    gap_log = decay_heads[:, :, None] - decay_heads[:, None, :]
    decays = jnp.exp(jnp.where(causal, gap_log, -jnp.inf))
    scores = jnp.einsum("tn,sn->ts", c_vals, b_vals, precision=lax.Precision.HIGHEST)
    weights = decays * scores[None, :, :] * dt_soft.T[:, None, :]
    inner = jnp.einsum("hts,shp->thp", weights, values, precision=lax.Precision.HIGHEST)
    outer = jnp.exp(log_decay)[:, :, None] * jnp.einsum(
        "tn,hpn->thp", c_vals, carry_in, precision=lax.Precision.HIGHEST
    )
    to_end = jnp.exp(log_decay[-1][None, :] - log_decay) * dt_soft
    carry_out = jnp.exp(log_decay[-1])[:, None, None] * carry_in + jnp.einsum(
        "sh,shp,sn->hpn", to_end, values, b_vals, precision=lax.Precision.HIGHEST
    )
    return (inner + outer, carry_out)


def affine_combine(earlier, later):
    return (earlier[0] * later[0], later[0][:, None, None] * earlier[1] + later[1])


def shards(layer_input, projection, ssm_input, step_logit, decay_rate, output_grad):
    tokens = layer_input[0]
    x_rows = ssm_input[0]
    logit_rows = step_logit[0]
    grad_rows = output_grad[0]
    row_count = x_rows.shape[0]
    head_count = logit_rows.shape[1]
    head_size = x_rows.shape[1] // head_count
    state_size = projection.shape[1] // 2
    projected = jnp.dot(tokens, projection, preferred_element_type=jnp.float32).astype(jnp.bfloat16)
    b_rows = projected[:, :state_size]
    c_rows = projected[:, state_size:]
    values = x_rows.astype(jnp.float32).reshape(row_count, head_count, head_size)
    dt_soft = jax.nn.softplus(logit_rows)
    log_decay = jnp.cumsum(-decay_rate[None, :] * dt_soft, axis=0)
    span_decay = jnp.exp(log_decay[-1])
    to_end = jnp.exp(log_decay[-1][None, :] - log_decay) * dt_soft
    local_state = jnp.einsum(
        "sh,shp,sn->hpn",
        to_end,
        values,
        b_rows.astype(jnp.float32),
        precision=lax.Precision.HIGHEST,
    )
    identity = (
        jnp.ones((head_count,), jnp.float32),
        jnp.zeros((head_count, head_size, state_size), jnp.float32),
    )
    entering = carried_in((span_decay, local_state), "seq", affine_combine, identity, False)[1]
    grad_vals = grad_rows.astype(jnp.float32).reshape(row_count, head_count, head_size)
    local_adjoint = jnp.einsum(
        "th,thp,tn->hpn",
        jnp.exp(log_decay),
        grad_vals,
        c_rows.astype(jnp.float32),
        precision=lax.Precision.HIGHEST,
    )
    leaving = carried_in((span_decay, local_adjoint), "seq", affine_combine, identity, True)[1]

    def forward_at(x_arg, b_arg, c_arg, logit_arg, rate_arg):
        return span_forward(x_arg, b_arg, c_arg, logit_arg, rate_arg, entering)

    unused, pullback = jax.vjp(forward_at, x_rows, b_rows, c_rows, logit_rows, decay_rate)
    grad_x, grad_b, grad_c, grad_logit, grad_rate = pullback((grad_vals, leaving))
    grad_bc = jnp.concatenate([grad_b, grad_c], axis=1)
    group_rows = lax.psum_scatter(
        lax.dot_general(
            tokens, grad_bc, (((0,), (0,)), ((), ())), preferred_element_type=jnp.float32
        ),
        "seq",
        scatter_dimension=0,
        tiled=True,
    )
    weight_rows = lax.psum(group_rows, "dp")
    rate_sum = lax.psum(grad_rate, ("seq", "dp"))
    return (grad_x[None], grad_logit[None], rate_sum, weight_rows)


def solution(mesh):
    placed = (
        P("dp", "seq", None),
        P(),
        P("dp", "seq", None),
        P("dp", "seq", None),
        P(),
        P("dp", "seq", None),
    )
    return jax.shard_map(
        shards,
        mesh=mesh,
        in_specs=placed,
        out_specs=(P("dp", "seq", None), P("dp", "seq", None), P(), P("seq", None)),
        check_vma=False,
    )
```

profile of v0, /device:TPU:0, one launch (start us, length us, event | category | flops | bytes accessed | tf_op | source)
XLA Modules:
  0.0 672.9 jit_solution(1227657317378317250)
XLA Ops:
  7.2 0.8 neg.23
  8.0 0.8 broadcast_multiply_fusion
  8.9 0.1 copy.51
  9.0 0.2 reduce_window_sum.24
  9.2 1.6 copy.54
  10.9 1.7 convolution_convert_fusion
  12.5 2.5 fusion.7
  15.1 0.2 slice_reduce_fusion
  15.3 22.7 %all-gather.2 = f32[8,1,64]{2,1,0:T(1,128)S(1)} all-gather(f32[1,1,64]{2,1,0:T(1,128)S(1)} %bitcast.131), channel_id=1, replica_groups=mesh['seq'=8,'dp'=4] {'seq'}, dimensions={0}, use_global_device_ids=true | all-gather | bytes 2304 | tf_op jit(solution)/shard_map/all_gather | solution.py:9
  38.0 2.3 copy.58
  40.3 204.9 %all-gather.6.cloned.1.call-done = f32[512,64,128]{2,1,0:T(8,128)} async-done(((f32[64,64,128]{2,1,0:T(8,128)}), f32[512,64,128]{2,1,0:T(8,128)}) %all-gather.6.cloned.1.call-update) | async-done | bytes 16777232 | tf_op jit(solution)/shard_map/all_gather | solution.py:9
  245.3 11.8 %rev.7 = f32[8,64,64,128]{3,2,1,0:T(8,128)} reverse(f32[8,64,64,128]{3,2,1,0:T(8,128)} %bitcast.123), dimensions={0} | reverse | bytes 33554432 | tf_op jit(solution)/shard_map/rev | solution.py:11
  257.0 14.8 %while.28 = (s32[]{:T(128)}, f32[64,64,128]{2,1,0:T(8,128)S(1)}, s32[]{:T(128)}, f32[8,64]{1,0:T(8,128)S(1)}, f32[8,64,64,128]{3,2,1,0:T(8,128)}, /*index=5*/s32[]{:T(128)}, s32[]{:T(128)}) while((s32[]{:T(128)}, f32[64,64,128]{2,1,0:T(8,128)S(1)}, s32[]{:T(128)}, f32[8,64]{1,0:T(8,128)S(1)}, f32[8,64,64,128]{3,2,1,0:T(8,128)}, ...), condition=%wide.region_2.3_spmd.clone, body=%wide.region_1.2_spmd.clone.sunk | while | flops 2097156 | bytes 6292329 | solution.py:21
  257.0 2.1 fusion.78
  259.2 2.1 fusion.78
  261.3 2.1 fusion.78
  263.4 2.1 fusion.78
  265.5 2.1 fusion.78
  267.7 2.1 fusion.78
  269.8 2.1 fusion.78
  271.9 4.4 fusion.13
  276.3 0.7 fusion.65
  277.0 2.5 fusion.9
  279.5 0.2 reduce-scatter.2.cloned.1.call-start
  279.8 0.7 copy.56
  280.5 0.1 fusion.55
  280.6 5.5 fusion.23
  286.2 4.6 fusion.11
  290.8 0.2 fusion.25
  291.0 214.2 %all-gather.8.cloned.1.call-done = f32[512,64,128]{2,1,0:T(8,128)} async-done(((f32[64,64,128]{2,1,0:T(8,128)}), f32[512,64,128]{2,1,0:T(8,128)}) %all-gather.8.cloned.1.call-update) | async-done | bytes 16777232 | tf_op jit(solution)/shard_map/all_gather | solution.py:9
  505.2 23.0 %while.29 = (s32[]{:T(128)}, f32[64,64,128]{2,1,0:T(8,128)S(1)}, s32[]{:T(128)}, f32[8,64]{1,0:T(8,128)}, f32[8,64,64,128]{3,2,1,0:T(8,128)}, /*index=5*/s32[]{:T(128)}, s32[]{:T(128)}) while((s32[]{:T(128)}, f32[64,64,128]{2,1,0:T(8,128)S(1)}, s32[]{:T(128)}, f32[8,64]{1,0:T(8,128)}, f32[8,64,64,128]{3,2,1,0:T(8,128)}, ...), condition=%wide.region_5.6_spmd.clone, body=%wide.region_4.5_spmd.clone.sunk | while | flops 2097156 | bytes 6292329 | solution.py:21
  505.2 1.2 dynamic-slice_bitcast_fusion.5
  506.4 2.1 fusion.79
  508.5 1.2 dynamic-slice_bitcast_fusion.5
  509.7 2.1 fusion.79
  511.8 1.2 dynamic-slice_bitcast_fusion.5
  513.0 2.1 fusion.79
  515.1 1.2 dynamic-slice_bitcast_fusion.5
  516.3 2.1 fusion.79
  518.4 1.2 dynamic-slice_bitcast_fusion.5
  519.6 2.1 fusion.79
  521.7 1.2 dynamic-slice_bitcast_fusion.5
  522.9 2.1 fusion.79
  524.9 1.2 dynamic-slice_bitcast_fusion.5
  526.1 2.1 fusion.79
  528.3 3.5 fusion.24
  531.8 0.2 fusion.26
  532.0 2.6 convolution_bitcast_fusion
  534.7 0.3 all-reduce.4.cloned.1.call-start
  535.0 0.4 copy-done.20
  535.3 0.1 copy.60
  535.5 5.6 fusion.14
  541.1 2.3 copy.64
  543.3 2.2 multiply_reduce_fusion.2
  545.5 0.1 copy.59
  545.6 0.1 fusion.50
  545.7 2.9 fusion.12
  548.6 73.2 %reduce-scatter.2.cloned.1.call-done = f32[512,256]{0,1:T(8,128)} async-done(((f32[4096,256]{0,1:T(8,128)}), f32[512,256]{0,1:T(8,128)}) %reduce-scatter.2.cloned.1.call-update) | async-done | bytes 524304 | tf_op jit(solution)/shard_map/reduce_scatter | solution.py:101
  621.8 0.1 bitcast_add_fusion.3
  621.9 0.1 copy.61
  622.0 1.1 reduce_window_sum.25
  623.2 0.8 multiply_reduce_fusion.3
  624.0 40.3 %psum.14 = f32[64]{0:T(128)} all-reduce(f32[64]{0:T(128)S(1)} %neg.27), channel_id=1, replica_groups=mesh['seq'=8,'dp'=4] {'seq','dp'}, use_global_device_ids=true, to_apply=%region_13.14 | all-reduce | flops 64 | bytes 512 | tf_op jit(solution)/shard_map/psum | solution.py:110
  664.3 2.0 copy.65
  (63 shorter events, 0.5 us)
Async XLA Ops:
  7.2 3.7 copy-start
  7.2 238.1 %all-gather.6.cloned.1.call-start = ((), (), s32[]{:S(2)}) async-start(), calls=%async_computation.3 | async-start | bytes 18874368 | tf_op jit(solution)/shard_map/all_gather | solution.py:9
  8.0 1.2 copy-start.18
  15.1 490.1 %all-gather.8.cloned.1.call-start = ((), (), s32[]{:S(2)}) async-start(), calls=%async_computation.4 | async-start | bytes 18874368 | tf_op jit(solution)/shard_map/all_gather | solution.py:9
  15.3 261.0 %copy-start.16 = (f32[64]{0:T(128)}, f32[64]{0:T(128)S(1)}, u32[]{:S(2)}) copy-start(f32[64]{0:T(128)S(1)} %get-tuple-element.250) | copy-start | bytes 772
  38.0 219.0 %copy-start.15 = (f32[8,1,64]{2,1,0:T(1,128)}, f32[8,1,64]{2,1,0:T(1,128)S(1)}, u32[]{:S(2)}) copy-start(f32[8,1,64]{2,1,0:T(1,128)S(1)} %all-gather.2) | copy-start | bytes 6148
  271.9 4.4 copy-start.3
  271.9 4.4 copy-start.7
  271.9 5.1 copy-start.4
  277.0 9.1 %copy-start.10 = (f32[64,128]{1,0:T(8,128)}, f32[64,128]{1,0:T(8,128)S(1)}, u32[]{:S(2)}) copy-start(f32[64,128]{1,0:T(8,128)S(1)} %get-tuple-element.276) | copy-start | bytes 98308
  279.5 342.2 %reduce-scatter.2.cloned.1.call-start = ((), (), s32[]{:S(2)}) async-start(), calls=%async_computation.1 | async-start | bytes 4718592 | tf_op jit(solution)/shard_map/reduce_scatter | solution.py:101
  280.5 5.7 copy-start.5
  280.5 5.7 copy-start.12
  528.2 15.1 %copy-start.2 = (f32[64,64,128]{2,1,0:T(8,128)}, f32[64,64,128]{2,1,0:T(8,128)S(1)}, u32[]{:S(2)}) copy-start(f32[64,64,128]{2,1,0:T(8,128)S(1)} %get-tuple-element.193) | copy-start | bytes 6291460
  528.2 3.8 copy-start.6
  534.7 0.7 copy-start.20
  534.7 0.8 copy-start.11
  534.7 0.8 copy-start.13
  534.7 129.6 %all-reduce.4.cloned.1.call-start = ((), (), s32[]{:S(2)}) async-start(), calls=%async_computation.2 | async-start | bytes 1048576 | tf_op jit(solution)/shard_map/psum | solution.py:109
  545.5 76.3 %copy-start.8 = (f32[64,128]{1,0:T(8,128)S(1)}, f32[64,128]{1,0:T(8,128)}, u32[]{:S(2)}) copy-start(f32[64,128]{1,0:T(8,128)} %get-tuple-element.246) | copy-start | bytes 98308
  545.5 76.3 %copy-start.9 = (f32[64,128]{1,0:T(8,128)S(1)}, f32[64,128]{1,0:T(8,128)}, u32[]{:S(2)}) copy-start(f32[64,128]{1,0:T(8,128)} %get-tuple-element.247) | copy-start | bytes 98308
  545.5 76.3 %copy-start.17 = (f32[64]{0:T(128)S(1)}, f32[64]{0:T(128)}, u32[]{:S(2)}) copy-start(f32[64]{0:T(128)} %copy-done.16) | copy-start | bytes 772
  545.6 120.8 %copy-start.1 = (bf16[4096,256]{1,0:T(8,128)(2,1)S(1)}, bf16[4096,256]{1,0:T(8,128)(2,1)}, u32[]{:S(2)}) copy-start(bf16[4096,256]{1,0:T(8,128)(2,1)} %param.11) | copy-start | bytes 6291460
  545.7 77.5 %copy-start.14 = (f32[64,128]{1,0:T(8,128)S(1)}, f32[64,128]{1,0:T(8,128)}, u32[]{:S(2)}) copy-start(f32[64,128]{1,0:T(8,128)} %get-tuple-element.248) | copy-start | bytes 98308
  545.7 77.5 %copy-start.19 = (f32[64]{0:T(128)S(1)}, f32[64]{0:T(128)}, u32[]{:S(2)}) copy-start(f32[64]{0:T(128)} %copy-done.18) | copy-start | bytes 772
Sparse Core Ops, SparseCore 0:
  15.2 230.0 all-gather.5
  279.7 225.5 all-gather.7
  534.8 86.8 reduce-scatter.1
  624.0 33.2 all-reduce.3
where the time goes:
time: 674 us; the launch traced here: 673 us
  waiting for transfers between devices  492 us (73%)
  blocking collectives  63 us (9%)
  matrix products  36.4 us (5%)
  other arithmetic  35.9 us (5%)
  local copies, waits for them, and re-layouts  30.2 us (4%)
  between operations  14.1 us (2%)
    all_gather x2, waiting for transfers between devices, carried_in(): pieces = jax.tree.map(lambda part: lax.all_gather(part, axis), value)  419 us
    reduce_scatter x1, waiting for transfers between devices, shards(): lax.psum_scatter(lax.dot_general(tokens, grad_bc, (((0,), (0,)), ((), ())...  73.2 us
    psum x1, blocking collectives, shards(): rate_sum = lax.psum(grad_rate, ('seq', 'dp'))  40.3 us
    select_n x14, other arithmetic, lap(): jnp.where(position < mine, new, old)  29.1 us
    all_gather x1, blocking collectives, carried_in(): pieces = jax.tree.map(lambda part: lax.all_gather(part, axis), value)  22.7 us
  transfers between devices with their start and end apart: 4, of which 3 were waited for; matrix products, arithmetic and copies ran while one was open for 4% of the time, Pallas kernels for 0%

commit v1 on v0

v1 whole, which is shorter than its diff:
```python
import functools

import jax
import jax.numpy as jnp
from jax import lax
from jax.experimental import pallas as pl
from jax.experimental.pallas import tpu as pltpu
from jax.sharding import PartitionSpec as P

F32 = jnp.float32
BF16 = jnp.bfloat16
HEADS = 8


def dot(a, b, ca, cb):
    return lax.dot_general(a, b, (((ca,), (cb,)), ((), ())), preferred_element_type=F32)


def pair_columns(cols, j, size):
    rows = cols.shape[0]
    lane = lax.broadcasted_iota(jnp.int32, (rows, 2 * size), 1)
    return jnp.where(lane < size, cols[:, j : j + 1], cols[:, j + 1 : j + 2])


def local_kernel(size, b_ref, c_ref, x_ref, g_ref, col_ref, s_ref, a_ref):
    cols = col_ref[0]
    width = 2 * size
    for pair in range(HEADS // 2):
        lanes = pl.ds(pair * width, width)
        j = 2 * pair
        to_end = pair_columns(cols, j + HEADS, size) * pair_columns(cols, j + 2 * HEADS, size)
        grow = pair_columns(cols, j + 3 * HEADS, size)
        xs = (x_ref[:, lanes].astype(F32) * to_end).astype(BF16)
        gs = (g_ref[:, lanes].astype(F32) * grow).astype(BF16)
        s_ref[0, :, lanes] = dot(b_ref[...], xs, 0, 0)
        a_ref[0, :, lanes] = dot(c_ref[...], gs, 0, 0)


def scan_kernel(
    n, d_ref, s_ref, a_ref, e_out, f_out,
    d_in, s_in, a_in, e_in, f_in, e_snd, f_snd,
    d_sem, s_sem, a_sem, e_sem, f_sem,
):
    chunks = s_ref.shape[0]
    nz = n // 2
    me = lax.axis_index("seq")
    odd = lax.rem(me, 2)
    z = lax.div(me, 2)
    partner = me + 1 - 2 * odd
    first, last = z == 0, z == nz - 1
    barrier = pltpu.get_barrier_semaphore()

    def greet(who):
        pl.semaphore_signal(
            barrier, inc=1, device_id={"seq": who}, device_id_type=pl.DeviceIdType.MESH
        )

    greet(partner)
    pl.when(jnp.logical_not(first))(lambda: greet(me - 2))
    pl.when(jnp.logical_not(last))(lambda: greet(me + 2))
    end = jnp.logical_or(first, last)
    pl.when(end)(lambda: pl.semaphore_wait(barrier, min(nz, 2)))
    pl.when(jnp.logical_not(end))(lambda: pl.semaphore_wait(barrier, 3))

    def send(src, dst, sems, k, who):
        return pltpu.make_async_remote_copy(
            src_ref=src, dst_ref=dst, send_sem=sems.at[0, k], recv_sem=sems.at[1, k],
            device_id={"seq": who}, device_id_type=pl.DeviceIdType.MESH,
        )

    def copy_d():
        return send(d_ref, d_in, d_sem, 0, partner)

    def copy_s(k):
        return send(s_ref.at[k], s_in.at[k], s_sem, k, partner)

    def copy_a(k):
        return send(a_ref.at[k], a_in.at[k], a_sem, k, partner)

    def copy_e(k):
        return send(e_snd.at[k], e_in.at[k], e_sem, k, me + 2)

    def copy_f(k):
        return send(f_snd.at[k], f_in.at[k], f_sem, k, me - 2)

    copy_d().start()
    for k in range(chunks):
        copy_s(k).start()
        copy_a(k).start()

    @pl.when(first)
    def _():
        e_in[...] = jnp.zeros_like(e_in)

    @pl.when(last)
    def _():
        f_in[...] = jnp.zeros_like(f_in)

    copy_d().wait_recv()

    def advance(k, near, far, carry, out, snd, near_first):
        @pl.when(near_first)
        def _():
            value = carry[k]
            out[k] = value.astype(out.dtype)
            middle = d_ref[k, 0:1] * value + near[k]
            snd[k] = d_in[k, 0:1] * middle + far[k]

        @pl.when(jnp.logical_not(near_first))
        def _():
            middle = d_in[k, 0:1] * carry[k] + far[k]
            out[k] = middle.astype(out.dtype)
            snd[k] = d_ref[k, 0:1] * middle + near[k]

    def step(t, unused):
        kf = t - z

        @pl.when(jnp.logical_and(kf >= 0, kf < chunks))
        def _():
            copy_s(kf).wait_recv()
            pl.when(jnp.logical_not(first))(lambda: copy_e(kf).wait_recv())
            advance(kf, s_ref, s_in, e_in, e_out, e_snd, odd == 0)
            pl.when(jnp.logical_not(last))(lambda: copy_e(kf).start())

        kb = t - (nz - 1 - z)

        @pl.when(jnp.logical_and(kb >= 0, kb < chunks))
        def _():
            copy_a(kb).wait_recv()
            pl.when(jnp.logical_not(last))(lambda: copy_f(kb).wait_recv())
            advance(kb, a_ref, a_in, f_in, f_out, f_snd, odd == 1)
            pl.when(jnp.logical_not(first))(lambda: copy_f(kb).start())

        return unused

    lax.fori_loop(0, chunks + nz - 1, step, 0)
    copy_d().wait_send()
    for k in range(chunks):
        copy_s(k).wait_send()
        copy_a(k).wait_send()

    @pl.when(jnp.logical_not(last))
    def _():
        for k in range(chunks):
            copy_e(k).wait_send()

    @pl.when(jnp.logical_not(first))
    def _():
        for k in range(chunks):
            copy_f(k).wait_send()


def grad_kernel(
    size, b_ref, c_ref, x_ref, g_ref, col_ref, row_ref, e_ref, f_ref,
    dx_ref, rows_ref, cols_ref, ef_ref, gbc_ref,
    scores, d_scores, d_b, d_c,
):
    group = pl.program_id(0)
    b, c = b_ref[...], c_ref[...]
    length = b.shape[0]
    width = 2 * size

    @pl.when(group == 0)
    def _():
        scores[...] = dot(b, c, 1, 1)
        d_scores[...] = jnp.zeros_like(d_scores)
        d_b[...] = jnp.zeros_like(d_b)
        d_c[...] = jnp.zeros_like(d_c)

    cols = col_ref[0]
    rows = row_ref[...]
    k_st = scores[...]
    causal = lax.broadcasted_iota(jnp.int32, (length, length), 1) >= lax.broadcasted_iota(
        jnp.int32, (length, length), 0
    )
    lane = lax.broadcasted_iota(jnp.int32, (length, width), 1)
    low = lane < size
    place = lax.broadcasted_iota(jnp.int32, (length, cols_ref.shape[2]), 1)
    result = jnp.zeros((length, cols_ref.shape[2]), F32)
    q_sum = d_scores[...]
    b_sum, c_sum = d_b[...], d_c[...]
    for pair in range(HEADS // 2):
        lanes = pl.ds(pair * width, width)
        x2, g2 = x_ref[:, lanes], g_ref[:, lanes]
        x2f, g2f = x2.astype(F32), g2.astype(F32)
        e2, f2 = e_ref[0, :, lanes], f_ref[0, :, lanes]
        j = 2 * pair
        dt2 = pair_columns(cols, j + HEADS, size)
        end2 = pair_columns(cols, j + 2 * HEADS, size)
        grow2 = pair_columns(cols, j + 3 * HEADS, size)
        g_low = jnp.where(low, g2, jnp.zeros_like(g2))
        g_high = jnp.where(low, jnp.zeros_like(g2), g2)
        g_both = jnp.concatenate([g_low, g_high], axis=0)
        gram = dot(x2, g_both, 1, 1)
        weights = []
        for side in range(2):
            h = j + side
            gap = rows[h : h + 1, :] - cols[:, h : h + 1]
            decay = jnp.exp(jnp.where(causal, gap, -jnp.inf))
            mg = decay * gram[:, side * length : (side + 1) * length]
            dt = cols[:, h + HEADS : h + HEADS + 1]
            q_sum = q_sum + mg * dt
            raw = mg * k_st
            rows_ref[h : h + 1, :] = jnp.sum(raw * dt, axis=0, keepdims=True)
            result = jnp.where(place == h, jnp.sum(raw, axis=1, keepdims=True), result)
            weights.append((decay * k_st).astype(BF16))
        z2 = dot(jnp.concatenate(weights, axis=1), g_both, 1, 0)
        z_in = dot(b, f2, 1, 0) * end2
        dx_ref[:, lanes] = (dt2 * (z2 + z_in)).astype(dx_ref.dtype)
        y_in = dot(c, e2, 1, 0) * grow2
        xz, gy = x2f * z_in, g2f * y_in
        zero = jnp.zeros_like(xz)
        for side in range(2):
            h = j + side
            mask = low if side == 0 else jnp.logical_not(low)
            xs = jnp.sum(jnp.where(mask, xz, zero), axis=1, keepdims=True)
            gs = jnp.sum(jnp.where(mask, gy, zero), axis=1, keepdims=True)
            result = jnp.where(place == h + HEADS, xs, result)
            result = jnp.where(place == h + 2 * HEADS, gs, result)
        ef_ref[0, :, lanes] = jnp.sum(e2.astype(F32) * f2.astype(F32), axis=0, keepdims=True)
        b_sum = b_sum + dot((x2f * (end2 * dt2)).astype(BF16), f2, 1, 1)
        c_sum = c_sum + dot((g2f * grow2).astype(BF16), e2, 1, 1)
    cols_ref[0] = result
    d_scores[...] = q_sum
    d_b[...] = b_sum
    d_c[...] = c_sum

    @pl.when(group == pl.num_programs(0) - 1)
    def _():
        dk = q_sum.astype(BF16)
        state = b.shape[1]
        gbc_ref[:, :state] = (b_sum + dot(dk, c, 1, 0)).astype(gbc_ref.dtype)
        gbc_ref[:, state:] = (c_sum + dot(dk, b, 0, 0)).astype(gbc_ref.dtype)


def shards(layer_input, projection, ssm_input, step_logit, decay_rate, output_grad):
    tokens, x_rows, logit, grad_rows = layer_input[0], ssm_input[0], step_logit[0], output_grad[0]
    length, full = x_rows.shape
    heads = logit.shape[1]
    size = full // heads
    state = projection.shape[1] // 2
    groups = heads // HEADS
    width = HEADS * size
    count = lax.axis_size("seq")
    projected = jnp.dot(tokens, projection, preferred_element_type=F32).astype(BF16)
    b_rows, c_rows = projected[:, :state], projected[:, state:]
    dt = jax.nn.softplus(logit)
    log_decay = jnp.cumsum(-decay_rate[None, :] * dt, axis=0)
    to_end = jnp.exp(log_decay[-1][None, :] - log_decay)
    grow = jnp.exp(log_decay)
    span = grow[-1]

    def by_group(value):
        return value.reshape(length, groups, HEADS).transpose(1, 0, 2)

    cols = jnp.concatenate([by_group(v) for v in (log_decay, dt, to_end, grow)], axis=2)
    span_rows = jnp.broadcast_to(
        jnp.broadcast_to(span.reshape(groups, 1, HEADS, 1), (groups, 1, HEADS, size)).reshape(
            groups, 1, width
        ),
        (groups, 8, width),
    )
    whole = lambda shape: pl.BlockSpec(shape, lambda i: (0,) * len(shape))
    lanes = pl.BlockSpec((length, width), lambda i: (0, i))
    slab = lambda *shape: pl.BlockSpec((1,) + shape, lambda i: (i, 0, 0))
    limit = 60 * 2**20
    states = jax.ShapeDtypeStruct((groups, state, width), F32)
    local_state, local_adjoint = pl.pallas_call(
        functools.partial(local_kernel, size),
        grid=(groups,),
        in_specs=[
            whole((length, state)), whole((length, state)), lanes, lanes,
            slab(length, 4 * HEADS),
        ],
        out_specs=[slab(state, width), slab(state, width)],
        out_shape=[states, states],
        name="local_states",
    )(b_rows, c_rows, x_rows, grad_rows, cols)

    half = jax.ShapeDtypeStruct((groups, state, width), BF16)
    vmem = pl.BlockSpec(memory_space=pltpu.VMEM)
    slots = pltpu.VMEM((groups, state, width), F32)
    entering, leaving = pl.pallas_call(
        functools.partial(scan_kernel, count),
        in_specs=[vmem] * 3,
        out_specs=[vmem] * 2,
        out_shape=[half, half],
        scratch_shapes=[pltpu.VMEM((groups, 8, width), F32)]
        + [slots] * 6
        + [pltpu.SemaphoreType.DMA((2, 1))]
        + [pltpu.SemaphoreType.DMA((2, groups))] * 4,
        compiler_params=pltpu.CompilerParams(
            collective_id=0, has_side_effects=True, vmem_limit_bytes=limit
        ),
        name="scan_states",
    )(span_rows, local_state, local_adjoint)

    grad_x, row_sums, col_sums, inner, grad_bc = pl.pallas_call(
        functools.partial(grad_kernel, size),
        grid=(groups,),
        in_specs=[
            whole((length, state)), whole((length, state)), lanes, lanes,
            slab(length, 4 * HEADS), pl.BlockSpec((HEADS, length), lambda i: (i, 0)),
            slab(state, width), slab(state, width),
        ],
        out_specs=[
            lanes, pl.BlockSpec((HEADS, length), lambda i: (i, 0)), slab(length, 128),
            slab(1, width), whole((length, 2 * state)),
        ],
        out_shape=[
            jax.ShapeDtypeStruct((length, full), BF16),
            jax.ShapeDtypeStruct((heads, length), F32),
            jax.ShapeDtypeStruct((groups, length, 128), F32),
            jax.ShapeDtypeStruct((groups, 1, width), F32),
            jax.ShapeDtypeStruct((length, 2 * state), BF16),
        ],
        scratch_shapes=[
            pltpu.VMEM((length, length), F32), pltpu.VMEM((length, length), F32),
            pltpu.VMEM((length, state), F32), pltpu.VMEM((length, state), F32),
        ],
        name="gradients",
    )(b_rows, c_rows, x_rows, grad_rows, cols, log_decay.T, entering, leaving)

    def head_columns(part):
        piece = col_sums[:, :, part * HEADS : (part + 1) * HEADS]
        return piece.transpose(1, 0, 2).reshape(length, heads)

    inside, x_in, g_in = head_columns(0), head_columns(1), head_columns(2)
    both = span * jnp.sum(inner.reshape(heads, size), axis=1)
    position = jnp.arange(length)
    earlier = (position[:, None] > position[None, :]).astype(F32)
    change = g_in + row_sums.T - dt * inside
    d_log = (
        both[None, :]
        + jnp.dot(earlier, dt * x_in, precision=lax.Precision.HIGHEST)
        + jnp.dot((position[:, None] <= position[None, :]).astype(F32), change, precision=lax.Precision.HIGHEST)
    )
    d_dt = inside + x_in - decay_rate[None, :] * d_log
    grad_logit = d_dt * jax.nn.sigmoid(logit)
    grad_rate = -jnp.sum(dt * d_log, axis=0)
    group_rows = lax.psum_scatter(
        dot(tokens, grad_bc, 0, 0), "seq", scatter_dimension=0, tiled=True
    )
    weight_rows = lax.psum(group_rows, "dp")
    rate_sum = lax.psum(grad_rate, ("seq", "dp"))
    return (grad_x[None], grad_logit[None], rate_sum, weight_rows)


def solution(mesh):
    placed = (
        P("dp", "seq", None),
        P(),
        P("dp", "seq", None),
        P("dp", "seq", None),
        P(),
        P("dp", "seq", None),
    )
    return jax.shard_map(
        shards,
        mesh=mesh,
        in_specs=placed,
        out_specs=(P("dp", "seq", None), P("dp", "seq", None), P(), P("seq", None)),
        check_vma=False,
    )
```

time: 674 us -> 302 us (0.45)
  waiting for transfers between devices: 492 us -> 82.2 us
  Pallas kernels: 0 us -> 147 us
  other arithmetic: 35.9 us -> 2.05 us
  matrix products: 36.4 us -> 6.29 us
  blocking collectives: 63 us -> 40.3 us
  local copies, waits for them, and re-layouts: 30.2 us -> 9.62 us
    all_gather x2 -> x0, waiting for transfers between devices: 419 us -> none  [carried_in(): pieces = jax.tree.map(lambda part: lax.all_gather(part, axis), value)]
    pallas_call x0 -> x3, Pallas kernels: none -> 147 us  [the longest x1 120 us: shards(): pl.pallas_call(functools.partial(scan_kernel, count), in_specs=[vmem] * 3...]
    dot_general x13 -> x4, matrix products: 36.4 us -> 6.29 us  [the longest x1 3.49 us: dot(): lax.dot_general(a, b, (((ca,), (cb,)), ((), ())), preferred_element_type=...]
    select_n x14 -> x0, other arithmetic: 29.1 us -> none  [lap(): jnp.where(position < mine, new, old)]
    all_gather x1 -> x0, blocking collectives: 22.7 us -> none  [carried_in(): pieces = jax.tree.map(lambda part: lax.all_gather(part, axis), value)]
    rev x2 -> x0, local copies, waits for them, and re-layouts: 11.8 us -> none  [carried_in(): pieces = jax.tree.map(lambda part: part[::-1], pieces)]
    reduce_scatter x1, waiting for transfers between devices: 73.2 us -> 82.2 us  [shards(): lax.psum_scatter(dot(tokens, grad_bc, 0, 0), 'seq', scatter_dimension=0,...]
    mul x15 -> x1, local copies, waits for them, and re-layouts: 8.48 us -> 0.09 us  [shards(): log_decay = jnp.cumsum(-decay_rate[None, :] * dt, axis=0)]
  transfers between devices with their start and end apart: 4 -> 2, of which waited for: 3 -> 1; matrix products, arithmetic and copies ran while one was open for 4% -> 2% of each run, Pallas kernels for 0% -> 0%
where the time goes in v1:
time: 302 us; the launch traced here: 301 us
  Pallas kernels  147 us (49%)
  waiting for transfers between devices  82.2 us (27%)
  blocking collectives  40.3 us (13%)
  between operations  14.2 us (5%)
  local copies, waits for them, and re-layouts  9.62 us (3%)
  matrix products  6.29 us (2%)
    pallas_call x1, Pallas kernels, shards(): pl.pallas_call(functools.partial(scan_kernel, count), in_specs=[vmem] * 3...  120 us
    reduce_scatter x1, waiting for transfers between devices, shards(): lax.psum_scatter(dot(tokens, grad_bc, 0, 0), 'seq', scatter_dimension=0,...  82.2 us
    psum x1, blocking collectives, shards(): rate_sum = lax.psum(grad_rate, ('seq', 'dp'))  40.3 us
    pallas_call x1, Pallas kernels, shards(): pl.pallas_call(functools.partial(grad_kernel, size), grid=(groups,), in_s...  17 us
    pallas_call x1, Pallas kernels, shards(): pl.pallas_call(functools.partial(local_kernel, size), grid=(groups,), in_...  9.27 us
  transfers between devices with their start and end apart: 2, of which 1 were waited for; matrix products, arithmetic and copies ran while one was open for 2% of the time, Pallas kernels for 0%

profile of v1, /device:TPU:0, one launch (start us, length us, event | category | flops | bytes accessed | tf_op | source)
XLA Modules:
  0.0 301.4 jit_solution(15606405568562245444)
XLA Ops:
  7.2 0.0 copy-start
  7.2 0.0 copy-start.4
  7.2 0.0 reduce-scatter.2.cloned.1.call-start
  7.2 0.8 neg.17
  8.0 0.8 broadcast_multiply_fusion
  8.9 0.1 copy.28
  9.0 0.2 reduce_window_sum.11
  9.2 0.1 copy.29
  9.2 0.0 copy-start.3
  9.3 0.1 broadcast_in_dim.12
  9.3 0.1 sub.17
  9.4 0.1 broadcast_in_dim.13
  9.5 0.1 broadcast_in_dim.14
  9.6 0.0 copy-done
  9.6 1.7 convolution_convert_fusion
  11.3 0.6 fusion.25
  11.9 0.0 copy-done.4
  11.9 0.1 fusion.15
  12.0 1.0 copy.32.col_ref
  13.0 0.0 copy-done.3
  13.0 9.3 %local_states.1 = (f32[8,128,512]{2,1,0:T(8,128)}, f32[8,128,512]{2,1,0:T(8,128)}) custom-call(bf16[128,128]{1,0:T(8,128)(2,1)} %get-tuple-element.42.b_ref, bf16[128,128]{1,0:T(8,128)(2,1)} %get-tuple-element.41.c_ref, bf16[128,4096]{1,0:T(8,128)(2,1)} %bitcast.129, bf16[128,4096]{1,0:T(8,128)(2,1)} %bitcast.131, f32[8,128,32]{2,1,0:T(8,128)} %copy.32.col_ref), custom_call_target="tpu_custom_call" | custom-call | tf_op jit(solution)/shard_map/local_states/pallas_call | solution.py:268
  22.3 0.7 broadcast_in_dim.30.d_ref
  22.9 120.4 %scan_states.1 = (bf16[8,128,512]{2,1,0:T(8,128)(2,1)}, bf16[8,128,512]{2,1,0:T(8,128)(2,1)}) custom-call(f32[8,8,512]{2,1,0:T(8,128)} %broadcast_in_dim.30.d_ref, f32[8,128,512]{2,1,0:T(8,128)} %get-tuple-element.13.s_ref, f32[8,128,512]{2,1,0:T(8,128)} %get-tuple-element.14.a_ref), custom_call_target="tpu_custom_call" | custom-call | tf_op jit(solution)/shard_map/scan_states/pallas_call | solution.py:283
  143.3 0.0 copy-start.2
  143.3 17.0 %gradients.1 = (bf16[128,4096]{1,0:T(8,128)(2,1)}, f32[64,128]{1,0:T(8,128)}, f32[8,128,128]{2,1,0:T(8,128)}, f32[8,1,512]{2,1,0:T(1,128)}, bf16[128,256]{1,0:T(8,128)(2,1)}) custom-call(bf16[128,128]{1,0:T(8,128)(2,1)} %get-tuple-element.42.b_ref, bf16[128,128]{1,0:T(8,128)(2,1)} %get-tuple-element.41.c_ref, bf16[128,4096]{1,0:T(8,128)(2,1)} %bitcast.130, ...), custom_call_target="tpu_custom_call" | custom-call | tf_op jit(solution)/shard_map/gradients/pallas_call | solution.py:298
  160.4 0.0 copy-done.2
  160.4 3.5 %convolution_bitcast_fusion = f32[4096,256]{0,1:T(8,128)} fusion(bf16[128,256]{1,0:T(8,128)(2,1)} %get-tuple-element.21, bf16[1,128,4096]{2,1,0:T(8,128)(2,1)S(1)} %copy-done.2), kind=kOutput, calls=%fused_computation | convolution fusion | flops 268435456 | bytes 5308416 | tf_op jit(solution)/shard_map/dot_general | solution.py:16
  163.9 0.0 copy-start.5
  163.9 0.0 copy-start.1
  163.9 0.0 reduce-scatter.2.cloned.1.call-update
  163.9 0.0 all-reduce.2.cloned.1.call-start
  164.0 0.6 copy-done.5
  164.6 0.1 reshape.48
  164.7 0.1 reduce_sum.20
  164.8 0.1 copy-done.1
  164.9 0.0 copy-start.6
  164.9 0.0 copy-start.7
  164.9 1.3 slice_bitcast_fusion
  166.3 1.2 copy.35
  167.5 1.2 copy.34
  168.7 0.2 copy.33
  168.9 82.2 %reduce-scatter.2.cloned.1.call-done = f32[512,256]{0,1:T(8,128)} async-done(((f32[4096,256]{0,1:T(8,128)}), f32[512,256]{0,1:T(8,128)}) %reduce-scatter.2.cloned.1.call-update) | async-done | bytes 524304 | tf_op jit(solution)/shard_map/reduce_scatter | solution.py:341
  251.0 0.0 all-reduce.2.cloned.1.call-update
  251.0 0.2 convolution_add_fusion.1
  251.3 0.0 copy-done.6
  251.3 0.0 copy-done.7
  251.3 0.9 multiply_reduce_fusion
  252.2 40.3 %psum.14 = f32[64]{0:T(128)} all-reduce(f32[64]{0:T(128)S(1)} %neg.21), channel_id=1, replica_groups=mesh['seq'=8,'dp'=4] {'seq','dp'}, use_global_device_ids=true, to_apply=%region_3.4 | all-reduce | flops 64 | bytes 512 | tf_op jit(solution)/shard_map/psum | solution.py:345
  292.5 0.0 all-reduce.2.cloned.1.call-done
  292.5 2.0 copy.36
  (5 shorter events, 0.1 us)
Async XLA Ops:
  7.2 2.4 copy-start
  7.2 4.7 %copy-start.4 = (f32[1,128,64]{1,2,0:T(8,128)S(1)}, f32[1,128,64]{1,2,0:T(8,128)}, u32[]{:S(2)}) copy-start(f32[1,128,64]{1,2,0:T(8,128)} %param.9) | copy-start | bytes 98308
  7.2 243.8 %reduce-scatter.2.cloned.1.call-start = ((), (), s32[]{:S(2)}) async-start(), calls=%async_computation.1 | async-start | bytes 4718592 | tf_op jit(solution)/shard_map/reduce_scatter | solution.py:341
  9.2 3.8 %copy-start.3 = (f32[128,64]{0,1:T(8,128)}, f32[128,64]{0,1:T(8,128)S(1)}, u32[]{:S(2)}) copy-start(f32[128,64]{0,1:T(8,128)S(1)} %copy.29) | copy-start | bytes 98308
  143.3 17.0 %copy-start.2 = (bf16[1,128,4096]{2,1,0:T(8,128)(2,1)S(1)}, bf16[1,128,4096]{2,1,0:T(8,128)(2,1)}, u32[]{:S(2)}) copy-start(bf16[1,128,4096]{2,1,0:T(8,128)(2,1)} %param.6) | copy-start | bytes 3145732
  163.9 0.7 copy-start.5
  163.9 1.1 copy-start.1
  163.9 128.6 %all-reduce.2.cloned.1.call-start = ((), (), s32[]{:S(2)}) async-start(), calls=%async_computation.2 | async-start | bytes 1048576 | tf_op jit(solution)/shard_map/psum | solution.py:344
  164.9 86.3 %copy-start.6 = (f32[64,128]{1,0:T(8,128)S(1)}, f32[64,128]{1,0:T(8,128)}, u32[]{:S(2)}) copy-start(f32[64,128]{1,0:T(8,128)} %get-tuple-element.20) | copy-start | bytes 98308
  164.9 86.3 %copy-start.7 = (f32[64]{0:T(128)S(1)}, f32[64]{0:T(128)}, u32[]{:S(2)}) copy-start(f32[64]{0:T(128)} %param.10) | copy-start | bytes 772
Sparse Core Ops, SparseCore 0:
  164.0 86.9 reduce-scatter.1
  253.4 33.0 all-reduce.1

commit v2 on v1

--- a/solution.py
+++ b/solution.py
@@ -233,6 +233,135 @@
         gbc_ref[:, state:] = (c_sum + dot(dk, b, 0, 0)).astype(gbc_ref.dtype)
 
 
+def reversed_bits(value, size):
+    out, left = 0, size
+    while left > 1:
+        out, value, left = 2 * out + value % 2, value // 2, left // 2
+    return out
+
+
+def weight_kernel(
+    n, m, t_ref, g_ref, rate_ref, out_ref, rate_out,
+    acc, got, ring, r_acc, r_got, sem, out_sem, r_sem,
+):
+    chunks, blocks, rows = acc.shape[0], acc.shape[1], acc.shape[2]
+    piece = chunks * rows
+    seq, dp = lax.axis_index("seq"), lax.axis_index("dp")
+    steps, bit = [], 1
+    while bit < m:
+        steps.append(("dp", bit, lax.rem(lax.div(dp, bit), 2)))
+        bit *= 2
+    bit = 1
+    while bit < n:
+        steps.append(("seq", bit, lax.rem(lax.div(seq, bit), 2)))
+        bit *= 2
+    count = len(steps)
+
+    def peer(s):
+        axis, bit, mine = steps[s]
+        return {axis: lax.axis_index(axis) + bit - 2 * bit * mine}
+
+    def dp_peer(k):
+        other, bit = dp, 1
+        while bit < m:
+            if k & bit:
+                other = other + bit - 2 * bit * lax.rem(lax.div(dp, bit), 2)
+            bit *= 2
+        return {"dp": other}
+
+    barrier = pltpu.get_barrier_semaphore()
+    friends = [dp_peer(k) for k in range(1, m)] + [
+        peer(s) for s in range(count) if steps[s][0] == "seq"
+    ]
+    for friend in friends:
+        pl.semaphore_signal(
+            barrier, inc=1, device_id=friend, device_id_type=pl.DeviceIdType.MESH
+        )
+
+    starts, base, width = [], 0, blocks
+    for s in range(count):
+        width //= 2
+        mine = steps[s][2]
+        starts.append((base + width * mine, base + width * (1 - mine), width))
+        base = base + width * mine
+    offsets, total = [], 0
+    for s in range(count):
+        offsets.append(total)
+        total += starts[s][2]
+
+    def copy(c, s):
+        keep, give, size = starts[s]
+        return pltpu.make_async_remote_copy(
+            src_ref=acc.at[c, pl.ds(give, size)],
+            dst_ref=got.at[c, pl.ds(offsets[s], size)],
+            send_sem=sem.at[0, c, s], recv_sem=sem.at[1, c, s],
+            device_id=peer(s), device_id_type=pl.DeviceIdType.MESH,
+        )
+
+    def rate_copy(s):
+        return pltpu.make_async_remote_copy(
+            src_ref=r_acc.at[s], dst_ref=r_got.at[s],
+            send_sem=r_sem.at[0, s], recv_sem=r_sem.at[1, s],
+            device_id=peer(s), device_id_type=pl.DeviceIdType.MESH,
+        )
+
+    def out_copy(c, k):
+        return pltpu.make_async_remote_copy(
+            src_ref=ring.at[0, c], dst_ref=ring.at[k, c],
+            send_sem=out_sem.at[0, c, k], recv_sem=out_sem.at[1, c, k],
+            device_id=dp_peer(k), device_id_type=pl.DeviceIdType.MESH,
+        )
+
+    g = g_ref[...]
+    r_acc[0] = rate_ref[...]
+    block = 128
+    for first in range(0, t_ref.shape[1], block):
+        product = dot(t_ref[:, first : first + block], g, 0, 0)
+        for part in range(0, block, rows):
+            row = first + part
+            owner, inner = row // (m * piece), row % (m * piece)
+            place = reversed_bits(inner // piece, m) * n + reversed_bits(owner, n)
+            acc[inner % piece // rows, place] = product[part : part + rows]
+    pl.semaphore_wait(barrier, len(friends))
+    for c in range(chunks):
+        copy(c, 0).start()
+    rate_copy(0).start()
+    for turn in range(chunks + count):
+        for c in range(chunks):
+            s = turn - c
+            if not 0 <= s < count:
+                continue
+            copy(c, s).wait_recv()
+            keep, give, size = starts[s]
+            value = acc[c, pl.ds(keep, size)] + got[c, pl.ds(offsets[s], size)]
+            if s + 1 < count:
+                acc[c, pl.ds(keep, size)] = value
+                copy(c, s + 1).start()
+            else:
+                ring[0, c] = value[0]
+                for k in range(1, m):
+                    out_copy(c, k).start()
+        if turn < count:
+            rate_copy(turn).wait_recv()
+            r_acc[turn + 1] = r_acc[turn] + r_got[turn]
+            if turn + 1 < count:
+                rate_copy(turn + 1).start()
+    rate_out[...] = r_acc[count]
+    for c in range(chunks):
+        for k in range(m):
+            if k > 0:
+                out_copy(c, k).wait_recv()
+            where = dp_peer(k)["dp"] if k > 0 else dp
+            out_ref[pl.ds(where * piece + c * rows, rows)] = ring[k, c]
+    for c in range(chunks):
+        for s in range(count):
+            copy(c, s).wait_send()
+        for k in range(1, m):
+            out_copy(c, k).wait_send()
+    for s in range(count):
+        rate_copy(s).wait_send()
+
+
 def shards(layer_input, projection, ssm_input, step_logit, decay_rate, output_grad):
     tokens, x_rows, logit, grad_rows = layer_input[0], ssm_input[0], step_logit[0], output_grad[0]
     length, full = x_rows.shape
@@ -338,11 +467,37 @@
     d_dt = inside + x_in - decay_rate[None, :] * d_log
     grad_logit = d_dt * jax.nn.sigmoid(logit)
     grad_rate = -jnp.sum(dt * d_log, axis=0)
-    group_rows = lax.psum_scatter(
-        dot(tokens, grad_bc, 0, 0), "seq", scatter_dimension=0, tiled=True
-    )
-    weight_rows = lax.psum(group_rows, "dp")
-    rate_sum = lax.psum(grad_rate, ("seq", "dp"))
+    members = lax.axis_size("dp")
+    blocks = count * members
+    piece = tokens.shape[1] // blocks
+    chunks = max(1, min(4, piece // 8))
+    rows = piece // chunks
+    levels = blocks.bit_length() - 1
+    rate_rows = jnp.pad(grad_rate.reshape(1, heads), ((0, 7), (0, 128 - heads)))
+    weight_rows, rate_sum = pl.pallas_call(
+        functools.partial(weight_kernel, count, members),
+        in_specs=[vmem] * 3,
+        out_specs=[vmem] * 2,
+        out_shape=[
+            jax.ShapeDtypeStruct((members * piece, 2 * state), F32),
+            jax.ShapeDtypeStruct((8, 128), F32),
+        ],
+        scratch_shapes=[
+            pltpu.VMEM((chunks, blocks, rows, 2 * state), F32),
+            pltpu.VMEM((chunks, blocks, rows, 2 * state), F32),
+            pltpu.VMEM((members, chunks, rows, 2 * state), F32),
+            pltpu.VMEM((levels + 1, 8, 128), F32),
+            pltpu.VMEM((levels, 8, 128), F32),
+            pltpu.SemaphoreType.DMA((2, chunks, levels)),
+            pltpu.SemaphoreType.DMA((2, chunks, members)),
+            pltpu.SemaphoreType.DMA((2, levels)),
+        ],
+        compiler_params=pltpu.CompilerParams(
+            collective_id=1, has_side_effects=True, vmem_limit_bytes=limit
+        ),
+        name="weight_gradient",
+    )(tokens, grad_bc, rate_rows)
+    rate_sum = rate_sum[0, :heads]
     return (grad_x[None], grad_logit[None], rate_sum, weight_rows)
 
 

time: 302 us -> 213 us (0.71)
  waiting for transfers between devices: 82.2 us -> 0 us
  Pallas kernels: 147 us -> 195 us
  blocking collectives: 40.3 us -> 0 us
  between operations: 14.2 us -> 0.77 us
  matrix products: 6.29 us -> 2.83 us
    reduce_scatter x1 -> x0, waiting for transfers between devices: 82.2 us -> none  [shards(): lax.psum_scatter(dot(tokens, grad_bc, 0, 0), 'seq', scatter_dimension=0,...]
    pallas_call x0 -> x1, Pallas kernels: none -> 48.8 us  [shards(): pl.pallas_call(functools.partial(weight_kernel, count, members), in_specs...]
    psum x1 -> x0, blocking collectives: 40.3 us -> none  [shards(): rate_sum = lax.psum(grad_rate, ('seq', 'dp'))]
    dot_general x1 -> x0, matrix products: 3.49 us -> none  [dot(): lax.dot_general(a, b, (((ca,), (cb,)), ((), ())), preferred_element_type=...]
  transfers between devices with their start and end apart: 2 -> 0, of which waited for: 1 -> 0; matrix products, arithmetic and copies ran while one was open for 2% -> 0% of each run, Pallas kernels for 0% -> 0%
where the time goes in v2:
time: 213 us; the launch traced here: 212 us
  Pallas kernels  195 us (92%)
  local copies, waits for them, and re-layouts  10.6 us (5%)
  matrix products  2.83 us (1%)
  other arithmetic  2.79 us (1%)
    pallas_call x1, Pallas kernels, shards(): pl.pallas_call(functools.partial(scan_kernel, count), in_specs=[vmem] * 3...  120 us
    pallas_call x1, Pallas kernels, shards(): pl.pallas_call(functools.partial(weight_kernel, count, members), in_specs...  48.8 us
    pallas_call x1, Pallas kernels, shards(): pl.pallas_call(functools.partial(grad_kernel, size), grid=(groups,), in_s...  16.9 us
    pallas_call x1, Pallas kernels, shards(): pl.pallas_call(functools.partial(local_kernel, size), grid=(groups,), in_...  9.27 us

profile of v2, /device:TPU:0, one launch (start us, length us, event | category | flops | bytes accessed | tf_op | source)
XLA Modules:
  0.0 212.4 jit_solution(2945071232888382071)
XLA Ops:
  0.6 0.0 copy-start
  0.6 0.0 copy-start.2
  0.7 0.8 neg.27
  1.5 0.8 broadcast_multiply_fusion
  2.3 0.1 copy.26
  2.4 0.2 reduce_window_sum.11
  2.6 0.1 broadcast_in_dim.12
  2.7 0.1 sub.17
  2.8 0.1 broadcast_in_dim.13
  2.8 0.1 broadcast_in_dim.14
  2.9 0.1 copy.27
  3.0 0.0 copy-start.1
  3.0 0.0 copy-done
  3.0 1.7 convolution_convert_fusion
  4.7 0.6 fusion.24
  5.3 0.0 copy-done.2
  5.3 0.1 fusion.13
  5.4 0.7 broadcast_in_dim.30.d_ref
  6.1 1.0 copy.30.col_ref
  7.1 0.0 copy-done.1
  7.1 9.3 %local_states.1 = (f32[8,128,512]{2,1,0:T(8,128)}, f32[8,128,512]{2,1,0:T(8,128)}) custom-call(bf16[128,128]{1,0:T(8,128)(2,1)} %get-tuple-element.34.b_ref, bf16[128,128]{1,0:T(8,128)(2,1)} %get-tuple-element.33.c_ref, bf16[128,4096]{1,0:T(8,128)(2,1)} %bitcast.129, bf16[128,4096]{1,0:T(8,128)(2,1)} %bitcast.131, f32[8,128,32]{2,1,0:T(8,128)} %copy.30.col_ref), custom_call_target="tpu_custom_call" | custom-call | tf_op jit(solution)/shard_map/local_states/pallas_call | solution.py:397
  16.4 120.4 %scan_states.1 = (bf16[8,128,512]{2,1,0:T(8,128)(2,1)}, bf16[8,128,512]{2,1,0:T(8,128)(2,1)}) custom-call(f32[8,8,512]{2,1,0:T(8,128)} %broadcast_in_dim.30.d_ref, f32[8,128,512]{2,1,0:T(8,128)} %get-tuple-element.15.s_ref, f32[8,128,512]{2,1,0:T(8,128)} %get-tuple-element.16.a_ref), custom_call_target="tpu_custom_call" | custom-call | tf_op jit(solution)/shard_map/scan_states/pallas_call | solution.py:412
  136.8 16.9 %gradients.1 = (bf16[128,4096]{1,0:T(8,128)(2,1)}, f32[64,128]{1,0:T(8,128)}, f32[8,128,128]{2,1,0:T(8,128)}, f32[8,1,512]{2,1,0:T(1,128)}, bf16[128,256]{1,0:T(8,128)(2,1)}) custom-call(bf16[128,128]{1,0:T(8,128)(2,1)} %get-tuple-element.34.b_ref, bf16[128,128]{1,0:T(8,128)(2,1)} %get-tuple-element.33.c_ref, bf16[128,4096]{1,0:T(8,128)(2,1)} %bitcast.130, ...), custom_call_target="tpu_custom_call" | custom-call | tf_op jit(solution)/shard_map/gradients/pallas_call | solution.py:427
  153.7 0.8 reduce.2
  154.5 0.1 reshape.57
  154.6 0.1 reduce_sum.20
  154.7 0.0 copy-start.3
  154.7 0.0 copy-start.4
  154.7 2.5 %slice_bitcast_fusion = (f32[128,8,8]{2,0,1:T(8,128)}, f32[128,8,8]{2,0,1:T(8,128)S(1)}, f32[128,8,8]{2,0,1:T(8,128)S(1)}) fusion(f32[8,128,128]{2,1,0:T(8,128)} %get-tuple-element.20), kind=kLoop, calls=%fused_computation.3 | loop fusion | bytes 196608 | tf_op jit(solution)/shard_map/transpose | solution.py:455
  157.2 1.2 copy.33
  158.4 0.2 copy.32
  158.6 0.2 convolution_add_fusion.1
  158.8 0.2 copy.31
  159.0 0.0 copy-done.3
  159.0 0.0 copy-done.4
  159.0 0.9 multiply_reduce_fusion
  159.9 0.6 pad.4.rate_ref
  160.5 48.8 %weight_gradient.1 = (f32[512,256]{1,0:T(8,128)}, f32[8,128]{1,0:T(8,128)}) custom-call(bf16[128,4096]{1,0:T(8,128)(2,1)} %bitcast.128, bf16[128,256]{1,0:T(8,128)(2,1)} %get-tuple-element.23.g_ref, f32[8,128]{1,0:T(8,128)} %pad.4.rate_ref), custom_call_target="tpu_custom_call" | custom-call | tf_op jit(solution)/shard_map/weight_gradient/pallas_call | solution.py:477
  209.4 1.2 slice_bitcast_fusion.3
  210.6 1.9 copy.35
  (4 shorter events, 0.1 us)
Async XLA Ops:
  0.6 2.4 %copy-start = (bf16[4096,256]{1,0:T(8,128)(2,1)S(1)}, bf16[4096,256]{1,0:T(8,128)(2,1)}, u32[]{:S(2)}) copy-start(bf16[4096,256]{1,0:T(8,128)(2,1)} %param.7) | copy-start | bytes 6291460
  0.6 4.7 %copy-start.2 = (f32[1,128,64]{1,2,0:T(8,128)S(1)}, f32[1,128,64]{1,2,0:T(8,128)}, u32[]{:S(2)}) copy-start(f32[1,128,64]{1,2,0:T(8,128)} %param.9) | copy-start | bytes 98308
  3.0 4.1 %copy-start.1 = (f32[128,64]{0,1:T(8,128)}, f32[128,64]{0,1:T(8,128)S(1)}, u32[]{:S(2)}) copy-start(f32[128,64]{0,1:T(8,128)S(1)} %copy.27) | copy-start | bytes 98308
  154.7 4.3 %copy-start.3 = (f32[64,128]{1,0:T(8,128)S(1)}, f32[64,128]{1,0:T(8,128)}, u32[]{:S(2)}) copy-start(f32[64,128]{1,0:T(8,128)} %get-tuple-element.22) | copy-start | bytes 98308
  154.7 4.3 %copy-start.4 = (f32[64]{0:T(128)S(1)}, f32[64]{0:T(128)}, u32[]{:S(2)}) copy-start(f32[64]{0:T(128)} %param.10) | copy-start | bytes 772

commit v3 on v2

--- a/solution.py
+++ b/solution.py
@@ -9,7 +9,7 @@
 
 F32 = jnp.float32
 BF16 = jnp.bfloat16
-HEADS = 8
+HEADS = 4
 
 
 def dot(a, b, ca, cb):
@@ -22,26 +22,18 @@
     return jnp.where(lane < size, cols[:, j : j + 1], cols[:, j + 1 : j + 2])
 
 
-def local_kernel(size, b_ref, c_ref, x_ref, g_ref, col_ref, s_ref, a_ref):
-    cols = col_ref[0]
-    width = 2 * size
-    for pair in range(HEADS // 2):
-        lanes = pl.ds(pair * width, width)
-        j = 2 * pair
-        to_end = pair_columns(cols, j + HEADS, size) * pair_columns(cols, j + 2 * HEADS, size)
-        grow = pair_columns(cols, j + 3 * HEADS, size)
-        xs = (x_ref[:, lanes].astype(F32) * to_end).astype(BF16)
-        gs = (g_ref[:, lanes].astype(F32) * grow).astype(BF16)
-        s_ref[0, :, lanes] = dot(b_ref[...], xs, 0, 0)
-        a_ref[0, :, lanes] = dot(c_ref[...], gs, 0, 0)
-
-
-def scan_kernel(
-    n, d_ref, s_ref, a_ref, e_out, f_out,
+def layer_kernel(
+    n, size, b_ref, c_ref, x_ref, g_ref, col_ref, row_ref, d_ref,
+    dx_ref, rows_ref, cols_ref, ef_ref, gbc_ref,
+    s_ref, a_ref, e_out, f_out, scores, d_scores, d_b, d_c,
     d_in, s_in, a_in, e_in, f_in, e_snd, f_snd,
     d_sem, s_sem, a_sem, e_sem, f_sem,
 ):
     chunks = s_ref.shape[0]
+    length = b_ref.shape[0]
+    state = b_ref.shape[1]
+    width = 2 * size
+    heads = chunks * HEADS
     nz = n // 2
     me = lax.axis_index("seq")
     odd = lax.rem(me, 2)
@@ -58,9 +50,6 @@
     greet(partner)
     pl.when(jnp.logical_not(first))(lambda: greet(me - 2))
     pl.when(jnp.logical_not(last))(lambda: greet(me + 2))
-    end = jnp.logical_or(first, last)
-    pl.when(end)(lambda: pl.semaphore_wait(barrier, min(nz, 2)))
-    pl.when(jnp.logical_not(end))(lambda: pl.semaphore_wait(barrier, 3))
 
     def send(src, dst, sems, k, who):
         return pltpu.make_async_remote_copy(
@@ -83,10 +72,36 @@
     def copy_f(k):
         return send(f_snd.at[k], f_in.at[k], f_sem, k, me - 2)
 
+    def pair_lanes(k, pair):
+        return pl.ds(pl.multiple_of(k * (HEADS * size) + pair * width, width), width)
+
+    def local(k, unused):
+        cols = col_ref[k]
+        for pair in range(HEADS // 2):
+            lanes = pl.ds(pair * width, width)
+            wide = pair_lanes(k, pair)
+            j = 2 * pair
+            to_end = pair_columns(cols, j + HEADS, size) * pair_columns(cols, j + 2 * HEADS, size)
+            grow = pair_columns(cols, j + 3 * HEADS, size)
+            xs = (x_ref[:, wide].astype(F32) * to_end).astype(BF16)
+            gs = (g_ref[:, wide].astype(F32) * grow).astype(BF16)
+            s_ref[k, :, lanes] = dot(b_ref[...], xs, 0, 0)
+            a_ref[k, :, lanes] = dot(c_ref[...], gs, 0, 0)
+
+        @pl.when(k > 0)
+        def _():
+            copy_s(k - 1).start()
+            copy_a(k - 1).start()
+
+        return unused
+
+    end = jnp.logical_or(first, last)
+    pl.when(end)(lambda: pl.semaphore_wait(barrier, min(nz, 2)))
+    pl.when(jnp.logical_not(end))(lambda: pl.semaphore_wait(barrier, 3))
     copy_d().start()
-    for k in range(chunks):
-        copy_s(k).start()
-        copy_a(k).start()
+    lax.fori_loop(0, chunks, local, 0)
+    copy_s(chunks - 1).start()
+    copy_a(chunks - 1).start()
 
     @pl.when(first)
     def _():
@@ -96,6 +111,12 @@
     def _():
         f_in[...] = jnp.zeros_like(f_in)
 
+    b, c = b_ref[...], c_ref[...]
+    scores[...] = dot(b, c, 1, 1)
+    d_scores[...] = jnp.zeros_like(d_scores)
+    d_b[...] = jnp.zeros_like(d_b)
+    d_c[...] = jnp.zeros_like(d_c)
+    cols_ref[...] = jnp.zeros_like(cols_ref)
     copy_d().wait_recv()
 
     def advance(k, near, far, carry, out, snd, near_first):
@@ -112,6 +133,67 @@
             out[k] = middle.astype(out.dtype)
             snd[k] = d_ref[k, 0:1] * middle + near[k]
 
+    def gradients(k):
+        cols = col_ref[k]
+        rows = row_ref[k]
+        k_st = scores[...]
+        causal = lax.broadcasted_iota(jnp.int32, (length, length), 1) >= lax.broadcasted_iota(
+            jnp.int32, (length, length), 0
+        )
+        low = lax.broadcasted_iota(jnp.int32, (length, width), 1) < size
+        place = lax.broadcasted_iota(jnp.int32, cols_ref.shape, 1) - k * HEADS
+        result = cols_ref[...]
+        q_sum = d_scores[...]
+        b_sum, c_sum = d_b[...], d_c[...]
+        for pair in range(HEADS // 2):
+            lanes = pl.ds(pair * width, width)
+            wide = pair_lanes(k, pair)
+            x2, g2 = x_ref[:, wide], g_ref[:, wide]
+            x2f, g2f = x2.astype(F32), g2.astype(F32)
+            e2, f2 = e_out[k, :, lanes], f_out[k, :, lanes]
+            j = 2 * pair
+            dt2 = pair_columns(cols, j + HEADS, size)
+            end2 = pair_columns(cols, j + 2 * HEADS, size)
+            grow2 = pair_columns(cols, j + 3 * HEADS, size)
+            g_low = jnp.where(low, g2, jnp.zeros_like(g2))
+            g_high = jnp.where(low, jnp.zeros_like(g2), g2)
+            g_both = jnp.concatenate([g_low, g_high], axis=0)
+            gram = dot(x2, g_both, 1, 1)
+            weights = []
+            for side in range(2):
+                h = j + side
+                gap = rows[h : h + 1, :] - cols[:, h : h + 1]
+                decay = jnp.exp(jnp.where(causal, gap, -jnp.inf))
+                mg = decay * gram[:, side * length : (side + 1) * length]
+                dt = cols[:, h + HEADS : h + HEADS + 1]
+                q_sum = q_sum + mg * dt
+                raw = mg * k_st
+                rows_ref[k, h : h + 1, :] = jnp.sum(raw * dt, axis=0, keepdims=True)
+                result = jnp.where(place == h, jnp.sum(raw, axis=1, keepdims=True), result)
+                weights.append((decay * k_st).astype(BF16))
+            z2 = dot(jnp.concatenate(weights, axis=1), g_both, 1, 0)
+            z_in = dot(b, f2, 1, 0) * end2
+            dx_ref[:, wide] = (dt2 * (z2 + z_in)).astype(dx_ref.dtype)
+            y_in = dot(c, e2, 1, 0) * grow2
+            xz, gy = x2f * z_in, g2f * y_in
+            zero = jnp.zeros_like(xz)
+            for side in range(2):
+                h = j + side
+                mask = low if side == 0 else jnp.logical_not(low)
+                xs = jnp.sum(jnp.where(mask, xz, zero), axis=1, keepdims=True)
+                gs = jnp.sum(jnp.where(mask, gy, zero), axis=1, keepdims=True)
+                result = jnp.where(place == h + heads, xs, result)
+                result = jnp.where(place == h + 2 * heads, gs, result)
+            ef_ref[k, :, lanes] = jnp.sum(
+                e2.astype(F32) * f2.astype(F32), axis=0, keepdims=True
+            )
+            b_sum = b_sum + dot((x2f * (end2 * dt2)).astype(BF16), f2, 1, 1)
+            c_sum = c_sum + dot((g2f * grow2).astype(BF16), e2, 1, 1)
+        cols_ref[...] = result
+        d_scores[...] = q_sum
+        d_b[...] = b_sum
+        d_c[...] = c_sum
+
     def step(t, unused):
         kf = t - z
 
@@ -131,106 +213,23 @@
             advance(kb, a_ref, a_in, f_in, f_out, f_snd, odd == 1)
             pl.when(jnp.logical_not(first))(lambda: copy_f(kb).start())
 
+        pl.when(t >= nz - 1)(lambda: gradients(t - (nz - 1)))
         return unused
 
     lax.fori_loop(0, chunks + nz - 1, step, 0)
+    dk = d_scores[...].astype(BF16)
+    gbc_ref[:, :state] = (d_b[...] + dot(dk, c, 1, 0)).astype(gbc_ref.dtype)
+    gbc_ref[:, state:] = (d_c[...] + dot(dk, b, 0, 0)).astype(gbc_ref.dtype)
     copy_d().wait_send()
-    for k in range(chunks):
+
+    def settle(k, unused):
         copy_s(k).wait_send()
         copy_a(k).wait_send()
-
-    @pl.when(jnp.logical_not(last))
-    def _():
-        for k in range(chunks):
-            copy_e(k).wait_send()
-
-    @pl.when(jnp.logical_not(first))
-    def _():
-        for k in range(chunks):
-            copy_f(k).wait_send()
-
-
-def grad_kernel(
-    size, b_ref, c_ref, x_ref, g_ref, col_ref, row_ref, e_ref, f_ref,
-    dx_ref, rows_ref, cols_ref, ef_ref, gbc_ref,
-    scores, d_scores, d_b, d_c,
-):
-    group = pl.program_id(0)
-    b, c = b_ref[...], c_ref[...]
-    length = b.shape[0]
-    width = 2 * size
-
-    @pl.when(group == 0)
-    def _():
-        scores[...] = dot(b, c, 1, 1)
-        d_scores[...] = jnp.zeros_like(d_scores)
-        d_b[...] = jnp.zeros_like(d_b)
-        d_c[...] = jnp.zeros_like(d_c)
-
-    cols = col_ref[0]
-    rows = row_ref[...]
-    k_st = scores[...]
-    causal = lax.broadcasted_iota(jnp.int32, (length, length), 1) >= lax.broadcasted_iota(
-        jnp.int32, (length, length), 0
-    )
-    lane = lax.broadcasted_iota(jnp.int32, (length, width), 1)
-    low = lane < size
-    place = lax.broadcasted_iota(jnp.int32, (length, cols_ref.shape[2]), 1)
-    result = jnp.zeros((length, cols_ref.shape[2]), F32)
-    q_sum = d_scores[...]
-    b_sum, c_sum = d_b[...], d_c[...]
-    for pair in range(HEADS // 2):
-        lanes = pl.ds(pair * width, width)
-        x2, g2 = x_ref[:, lanes], g_ref[:, lanes]
-        x2f, g2f = x2.astype(F32), g2.astype(F32)
-        e2, f2 = e_ref[0, :, lanes], f_ref[0, :, lanes]
-        j = 2 * pair
-        dt2 = pair_columns(cols, j + HEADS, size)
-        end2 = pair_columns(cols, j + 2 * HEADS, size)
-        grow2 = pair_columns(cols, j + 3 * HEADS, size)
-        g_low = jnp.where(low, g2, jnp.zeros_like(g2))
-        g_high = jnp.where(low, jnp.zeros_like(g2), g2)
-        g_both = jnp.concatenate([g_low, g_high], axis=0)
-        gram = dot(x2, g_both, 1, 1)
-        weights = []
-        for side in range(2):
-            h = j + side
-            gap = rows[h : h + 1, :] - cols[:, h : h + 1]
-            decay = jnp.exp(jnp.where(causal, gap, -jnp.inf))
-            mg = decay * gram[:, side * length : (side + 1) * length]
-            dt = cols[:, h + HEADS : h + HEADS + 1]
-            q_sum = q_sum + mg * dt
-            raw = mg * k_st
-            rows_ref[h : h + 1, :] = jnp.sum(raw * dt, axis=0, keepdims=True)
-            result = jnp.where(place == h, jnp.sum(raw, axis=1, keepdims=True), result)
-            weights.append((decay * k_st).astype(BF16))
-        z2 = dot(jnp.concatenate(weights, axis=1), g_both, 1, 0)
-        z_in = dot(b, f2, 1, 0) * end2
-        dx_ref[:, lanes] = (dt2 * (z2 + z_in)).astype(dx_ref.dtype)
-        y_in = dot(c, e2, 1, 0) * grow2
-        xz, gy = x2f * z_in, g2f * y_in
-        zero = jnp.zeros_like(xz)
-        for side in range(2):
-            h = j + side
-            mask = low if side == 0 else jnp.logical_not(low)
-            xs = jnp.sum(jnp.where(mask, xz, zero), axis=1, keepdims=True)
-            gs = jnp.sum(jnp.where(mask, gy, zero), axis=1, keepdims=True)
-            result = jnp.where(place == h + HEADS, xs, result)
-            result = jnp.where(place == h + 2 * HEADS, gs, result)
-        ef_ref[0, :, lanes] = jnp.sum(e2.astype(F32) * f2.astype(F32), axis=0, keepdims=True)
-        b_sum = b_sum + dot((x2f * (end2 * dt2)).astype(BF16), f2, 1, 1)
-        c_sum = c_sum + dot((g2f * grow2).astype(BF16), e2, 1, 1)
-    cols_ref[0] = result
-    d_scores[...] = q_sum
-    d_b[...] = b_sum
-    d_c[...] = c_sum
-
-    @pl.when(group == pl.num_programs(0) - 1)
-    def _():
-        dk = q_sum.astype(BF16)
-        state = b.shape[1]
-        gbc_ref[:, :state] = (b_sum + dot(dk, c, 1, 0)).astype(gbc_ref.dtype)
-        gbc_ref[:, state:] = (c_sum + dot(dk, b, 0, 0)).astype(gbc_ref.dtype)
+        pl.when(jnp.logical_not(last))(lambda: copy_e(k).wait_send())
+        pl.when(jnp.logical_not(first))(lambda: copy_f(k).wait_send())
+        return unused
+
+    lax.fori_loop(0, chunks, settle, 0)
 
 
 def reversed_bits(value, size):
@@ -389,72 +388,38 @@
         ),
         (groups, 8, width),
     )
-    whole = lambda shape: pl.BlockSpec(shape, lambda i: (0,) * len(shape))
-    lanes = pl.BlockSpec((length, width), lambda i: (0, i))
-    slab = lambda *shape: pl.BlockSpec((1,) + shape, lambda i: (i, 0, 0))
     limit = 60 * 2**20
-    states = jax.ShapeDtypeStruct((groups, state, width), F32)
-    local_state, local_adjoint = pl.pallas_call(
-        functools.partial(local_kernel, size),
-        grid=(groups,),
-        in_specs=[
-            whole((length, state)), whole((length, state)), lanes, lanes,
-            slab(length, 4 * HEADS),
-        ],
-        out_specs=[slab(state, width), slab(state, width)],
-        out_shape=[states, states],
-        name="local_states",
-    )(b_rows, c_rows, x_rows, grad_rows, cols)
-
-    half = jax.ShapeDtypeStruct((groups, state, width), BF16)
     vmem = pl.BlockSpec(memory_space=pltpu.VMEM)
     slots = pltpu.VMEM((groups, state, width), F32)
-    entering, leaving = pl.pallas_call(
-        functools.partial(scan_kernel, count),
-        in_specs=[vmem] * 3,
-        out_specs=[vmem] * 2,
-        out_shape=[half, half],
-        scratch_shapes=[pltpu.VMEM((groups, 8, width), F32)]
+    half = pltpu.VMEM((groups, state, width), BF16)
+    square = pltpu.VMEM((length, length), F32)
+    sums = pltpu.VMEM((length, state), F32)
+    grad_x, row_sums, col_sums, inner, grad_bc = pl.pallas_call(
+        functools.partial(layer_kernel, count, size),
+        in_specs=[vmem] * 7,
+        out_specs=[vmem] * 5,
+        out_shape=[
+            jax.ShapeDtypeStruct((length, full), BF16),
+            jax.ShapeDtypeStruct((groups, HEADS, length), F32),
+            jax.ShapeDtypeStruct((length, 3 * heads), F32),
+            jax.ShapeDtypeStruct((groups, 1, width), F32),
+            jax.ShapeDtypeStruct((length, 2 * state), BF16),
+        ],
+        scratch_shapes=[slots, slots, half, half, square, square, sums, sums]
+        + [pltpu.VMEM((groups, 8, width), F32)]
         + [slots] * 6
         + [pltpu.SemaphoreType.DMA((2, 1))]
         + [pltpu.SemaphoreType.DMA((2, groups))] * 4,
         compiler_params=pltpu.CompilerParams(
             collective_id=0, has_side_effects=True, vmem_limit_bytes=limit
         ),
-        name="scan_states",
-    )(span_rows, local_state, local_adjoint)
-
-    grad_x, row_sums, col_sums, inner, grad_bc = pl.pallas_call(
-        functools.partial(grad_kernel, size),
-        grid=(groups,),
-        in_specs=[
-            whole((length, state)), whole((length, state)), lanes, lanes,
-            slab(length, 4 * HEADS), pl.BlockSpec((HEADS, length), lambda i: (i, 0)),
-            slab(state, width), slab(state, width),
-        ],
-        out_specs=[
-            lanes, pl.BlockSpec((HEADS, length), lambda i: (i, 0)), slab(length, 128),
-            slab(1, width), whole((length, 2 * state)),
-        ],
-        out_shape=[
-            jax.ShapeDtypeStruct((length, full), BF16),
-            jax.ShapeDtypeStruct((heads, length), F32),
-            jax.ShapeDtypeStruct((groups, length, 128), F32),
-            jax.ShapeDtypeStruct((groups, 1, width), F32),
-            jax.ShapeDtypeStruct((length, 2 * state), BF16),
-        ],
-        scratch_shapes=[
-            pltpu.VMEM((length, length), F32), pltpu.VMEM((length, length), F32),
-            pltpu.VMEM((length, state), F32), pltpu.VMEM((length, state), F32),
-        ],
-        name="gradients",
-    )(b_rows, c_rows, x_rows, grad_rows, cols, log_decay.T, entering, leaving)
-
-    def head_columns(part):
-        piece = col_sums[:, :, part * HEADS : (part + 1) * HEADS]
-        return piece.transpose(1, 0, 2).reshape(length, heads)
-
-    inside, x_in, g_in = head_columns(0), head_columns(1), head_columns(2)
+        name="layer_gradients",
+    )(
+        b_rows, c_rows, x_rows, grad_rows, cols,
+        log_decay.T.reshape(groups, HEADS, length), span_rows,
+    )
+    row_sums = row_sums.reshape(heads, length)
+    inside, x_in, g_in = (col_sums[:, i * heads : (i + 1) * heads] for i in range(3))
     both = span * jnp.sum(inner.reshape(heads, size), axis=1)
     position = jnp.arange(length)
     earlier = (position[:, None] > position[None, :]).astype(F32)

time: 213 us -> 181 us (0.85)
  Pallas kernels: 195 us -> 163 us
    pallas_call x3 -> x1, Pallas kernels: 147 us -> 116 us  [shards(): pl.pallas_call(functools.partial(layer_kernel, count, size), in_specs=[vm...]
    transpose x4 -> x1, local copies, waits for them, and re-layouts: 4.04 us -> 0.72 us  [shards(): log_decay.T.reshape(groups, HEADS, length)]
where the time goes in v3:
time: 181 us; the launch traced here: 180 us
  Pallas kernels  163 us (90%)
  local copies, waits for them, and re-layouts  9.86 us (5%)
  matrix products  4 us (2%)
  other arithmetic  2.12 us (1%)
    pallas_call x1, Pallas kernels, shards(): pl.pallas_call(functools.partial(layer_kernel, count, size), in_specs=[vm...  116 us
    pallas_call x1, Pallas kernels, shards(): pl.pallas_call(functools.partial(weight_kernel, count, members), in_specs...  47.6 us

profile of v3, /device:TPU:0, one launch (start us, length us, event | category | flops | bytes accessed | tf_op | source)
XLA Modules:
  0.0 180.0 jit_solution(746389676414987281)
XLA Ops:
  0.6 0.0 copy-start
  0.6 0.0 copy-start.3
  0.7 0.8 neg.27
  1.5 0.8 copy.31
  2.4 0.2 reduce_window_sum.11
  2.6 0.1 broadcast_in_dim.12
  2.7 0.1 sub.17
  2.7 0.1 broadcast_in_dim.13
  2.8 0.1 broadcast_in_dim.14
  2.9 0.1 copy.32
  3.0 0.7 copy.33
  3.7 0.0 copy-done
  3.7 1.7 convolution_convert_fusion
  5.4 0.6 fusion.20
  6.0 0.0 copy-done.3
  6.0 0.1 exponential_bitcast_fusion.1
  6.1 0.7 broadcast_in_dim.30.d_ref
  6.8 1.3 copy.34.col_ref
  8.1 0.0 copy-start.4
  8.1 115.7 %layer_gradients.1 = (bf16[128,4096]{1,0:T(8,128)(2,1)}, f32[16,4,128]{2,1,0:T(4,128)}, f32[128,192]{1,0:T(8,128)}, f32[16,1,256]{2,1,0:T(1,128)}, bf16[128,256]{1,0:T(8,128)(2,1)}) custom-call(bf16[128,128]{1,0:T(8,128)(2,1)} %get-tuple-element.35.b_ref, bf16[128,128]{1,0:T(8,128)(2,1)} %get-tuple-element.34.c_ref, bf16[128,4096]{1,0:T(8,128)(2,1)} %bitcast.79, ...), custom_call_target="tpu_custom_call" | custom-call | tf_op jit(solution)/shard_map/layer_gradients/pallas_call | solution.py:397
  123.8 0.0 copy-start.1
  123.8 0.8 reduce.2
  124.6 0.1 reshape.53
  124.7 0.1 reduce_sum.20
  124.8 1.1 convolution_add_fusion.1
  126.0 0.8 copy.36
  126.8 0.0 copy-done.4
  126.8 1.2 multiply_reduce_fusion
  128.1 0.6 pad.4.rate_ref
  128.7 0.7 copy.38
  129.4 47.6 %weight_gradient.1 = (f32[512,256]{1,0:T(8,128)}, f32[8,128]{1,0:T(8,128)}) custom-call(bf16[128,4096]{1,0:T(8,128)(2,1)} %bitcast.78, bf16[128,256]{1,0:T(8,128)(2,1)} %get-tuple-element.15.g_ref, f32[8,128]{1,0:T(8,128)} %pad.4.rate_ref), custom_call_target="tpu_custom_call" | custom-call | tf_op jit(solution)/shard_map/weight_gradient/pallas_call | solution.py:442
  177.0 0.0 copy-start.2
  177.0 1.2 slice_bitcast_fusion
  178.2 0.0 copy-done.1
  178.2 1.0 copy.43
  179.2 0.0 copy-done.2
  179.2 0.8 copy.44
  (5 shorter events, 0.1 us)
Async XLA Ops:
  0.6 3.1 %copy-start = (bf16[4096,256]{1,0:T(8,128)(2,1)S(1)}, bf16[4096,256]{1,0:T(8,128)(2,1)}, u32[]{:S(2)}) copy-start(bf16[4096,256]{1,0:T(8,128)(2,1)} %param.7) | copy-start | bytes 6291460
  0.6 5.4 %copy-start.3 = (f32[1,128,64]{1,2,0:T(8,128)S(1)}, f32[1,128,64]{1,2,0:T(8,128)}, u32[]{:S(2)}) copy-start(f32[1,128,64]{1,2,0:T(8,128)} %param.9) | copy-start | bytes 98308
  8.1 118.7 %copy-start.4 = (f32[64]{0:T(128)S(1)}, f32[64]{0:T(128)}, u32[]{:S(2)}) copy-start(f32[64]{0:T(128)} %param.10) | copy-start | bytes 772
  123.8 54.4 %copy-start.1 = (bf16[128,4096]{1,0:T(8,128)(2,1)S(1)}, bf16[128,4096]{1,0:T(8,128)(2,1)}, u32[]{:S(2)}) copy-start(bf16[128,4096]{1,0:T(8,128)(2,1)} %get-tuple-element.11) | copy-start | bytes 3145732
  177.0 2.2 %copy-start.2 = (f32[512,256]{1,0:T(8,128)S(1)}, f32[512,256]{1,0:T(8,128)}, u32[]{:S(2)}) copy-start(f32[512,256]{1,0:T(8,128)} %get-tuple-element.46) | copy-start | bytes 1572868

commit v4 on v3

--- a/solution.py
+++ b/solution.py
@@ -232,13 +232,6 @@
     lax.fori_loop(0, chunks, settle, 0)
 
 
-def reversed_bits(value, size):
-    out, left = 0, size
-    while left > 1:
-        out, value, left = 2 * out + value % 2, value // 2, left // 2
-    return out
-
-
 def weight_kernel(
     n, m, t_ref, g_ref, rate_ref, out_ref, rate_out,
     acc, got, ring, r_acc, r_got, sem, out_sem, r_sem,
@@ -246,18 +239,19 @@
     chunks, blocks, rows = acc.shape[0], acc.shape[1], acc.shape[2]
     piece = chunks * rows
     seq, dp = lax.axis_index("seq"), lax.axis_index("dp")
-    steps, bit = [], 1
+    dp_steps, seq_steps, bit = [], [], 1
     while bit < m:
-        steps.append(("dp", bit, lax.rem(lax.div(dp, bit), 2)))
+        dp_steps.append(("dp", bit, lax.rem(lax.div(dp, bit), 2)))
         bit *= 2
     bit = 1
     while bit < n:
-        steps.append(("seq", bit, lax.rem(lax.div(seq, bit), 2)))
+        seq_steps.append(("seq", bit, lax.rem(lax.div(seq, bit), 2)))
         bit *= 2
-    count = len(steps)
-
-    def peer(s):
-        axis, bit, mine = steps[s]
+    count = len(dp_steps) + len(seq_steps)
+    orders = (dp_steps + seq_steps, dp_steps[:1] + seq_steps + dp_steps[1:])
+
+    def peer(c, s):
+        axis, bit, mine = orders[c % 2][s]
         return {axis: lax.axis_index(axis) + bit - 2 * bit * mine}
 
     def dp_peer(k):
@@ -270,38 +264,39 @@
 
     barrier = pltpu.get_barrier_semaphore()
     friends = [dp_peer(k) for k in range(1, m)] + [
-        peer(s) for s in range(count) if steps[s][0] == "seq"
+        peer(0, s) for s in range(len(dp_steps), count)
     ]
     for friend in friends:
         pl.semaphore_signal(
             barrier, inc=1, device_id=friend, device_id_type=pl.DeviceIdType.MESH
         )
 
-    starts, base, width = [], 0, blocks
-    for s in range(count):
-        width //= 2
-        mine = steps[s][2]
-        starts.append((base + width * mine, base + width * (1 - mine), width))
-        base = base + width * mine
-    offsets, total = [], 0
-    for s in range(count):
-        offsets.append(total)
-        total += starts[s][2]
+    starts, offsets = [], []
+    for order in orders:
+        base, width, total = 0, blocks, 0
+        starts.append([])
+        for unused, unused, mine in order:
+            width //= 2
+            starts[-1].append((base + width * mine, base + width * (1 - mine), width))
+            base = base + width * mine
+            if len(starts) == 1:
+                offsets.append(total)
+                total += width
 
     def copy(c, s):
-        keep, give, size = starts[s]
+        keep, give, size = starts[c % 2][s]
         return pltpu.make_async_remote_copy(
             src_ref=acc.at[c, pl.ds(give, size)],
             dst_ref=got.at[c, pl.ds(offsets[s], size)],
             send_sem=sem.at[0, c, s], recv_sem=sem.at[1, c, s],
-            device_id=peer(s), device_id_type=pl.DeviceIdType.MESH,
+            device_id=peer(c, s), device_id_type=pl.DeviceIdType.MESH,
         )
 
     def rate_copy(s):
         return pltpu.make_async_remote_copy(
             src_ref=r_acc.at[s], dst_ref=r_got.at[s],
             send_sem=r_sem.at[0, s], recv_sem=r_sem.at[1, s],
-            device_id=peer(s), device_id_type=pl.DeviceIdType.MESH,
+            device_id=peer(0, s), device_id_type=pl.DeviceIdType.MESH,
         )
 
     def out_copy(c, k):
@@ -319,8 +314,11 @@
         for part in range(0, block, rows):
             row = first + part
             owner, inner = row // (m * piece), row % (m * piece)
-            place = reversed_bits(inner // piece, m) * n + reversed_bits(owner, n)
-            acc[inner % piece // rows, place] = product[part : part + rows]
+            chunk, place = inner % piece // rows, 0
+            for axis, bit, unused in orders[chunk % 2]:
+                index = inner // piece if axis == "dp" else owner
+                place = 2 * place + index // bit % 2
+            acc[chunk, place] = product[part : part + rows]
     pl.semaphore_wait(barrier, len(friends))
     for c in range(chunks):
         copy(c, 0).start()
@@ -331,7 +329,7 @@
             if not 0 <= s < count:
                 continue
             copy(c, s).wait_recv()
-            keep, give, size = starts[s]
+            keep, give, size = starts[c % 2][s]
             value = acc[c, pl.ds(keep, size)] + got[c, pl.ds(offsets[s], size)]
             if s + 1 < count:
                 acc[c, pl.ds(keep, size)] = value
@@ -435,7 +433,7 @@
     members = lax.axis_size("dp")
     blocks = count * members
     piece = tokens.shape[1] // blocks
-    chunks = max(1, min(4, piece // 8))
+    chunks = max(1, min(8, piece // 8))
     rows = piece // chunks
     levels = blocks.bit_length() - 1
     rate_rows = jnp.pad(grad_rate.reshape(1, heads), ((0, 7), (0, 128 - heads)))

time: 181 us -> 189 us (1.044)
  Pallas kernels: 163 us -> 172 us
    pallas_call x1, Pallas kernels: 47.6 us -> 56.6 us  [shards(): pl.pallas_call(functools.partial(weight_kernel, count, members), in_specs...]
where the time goes in v4:
time: 189 us
  Pallas kernels  172 us (91%)
  local copies, waits for them, and re-layouts  9.86 us (5%)
  matrix products  4 us (2%)
  other arithmetic  2.12 us (1%)
    pallas_call x1, Pallas kernels, shards(): pl.pallas_call(functools.partial(layer_kernel, count, size), in_specs=[vm...  116 us
    pallas_call x1, Pallas kernels, shards(): pl.pallas_call(functools.partial(weight_kernel, count, members), in_specs...  56.6 us

profile of v4, /device:TPU:0, one launch (start us, length us, event | category | flops | bytes accessed | tf_op | source)
XLA Modules:
  0.0 189.0 jit_solution(15485922213091597878)
XLA Ops:
  0.6 0.0 copy-start
  0.6 0.0 copy-start.3
  0.7 0.8 neg.27
  1.5 0.8 copy.31
  2.4 0.2 reduce_window_sum.11
  2.6 0.1 broadcast_in_dim.12
  2.7 0.1 sub.17
  2.7 0.1 broadcast_in_dim.13
  2.8 0.1 broadcast_in_dim.14
  2.9 0.1 copy.32
  3.0 0.7 copy.33
  3.7 0.0 copy-done
  3.7 1.7 convolution_convert_fusion
  5.4 0.6 fusion.20
  6.0 0.0 copy-done.3
  6.0 0.1 exponential_bitcast_fusion.1
  6.1 0.7 broadcast_in_dim.30.d_ref
  6.8 1.3 copy.34.col_ref
  8.1 0.0 copy-start.4
  8.1 115.7 %layer_gradients.1 = (bf16[128,4096]{1,0:T(8,128)(2,1)}, f32[16,4,128]{2,1,0:T(4,128)}, f32[128,192]{1,0:T(8,128)}, f32[16,1,256]{2,1,0:T(1,128)}, bf16[128,256]{1,0:T(8,128)(2,1)}) custom-call(bf16[128,128]{1,0:T(8,128)(2,1)} %get-tuple-element.35.b_ref, bf16[128,128]{1,0:T(8,128)(2,1)} %get-tuple-element.34.c_ref, bf16[128,4096]{1,0:T(8,128)(2,1)} %bitcast.79, ...), custom_call_target="tpu_custom_call" | custom-call | tf_op jit(solution)/shard_map/layer_gradients/pallas_call | solution.py:395
  123.8 0.0 copy-start.1
  123.8 0.8 reduce.2
  124.6 0.1 reshape.53
  124.7 0.1 reduce_sum.20
  124.8 1.1 convolution_add_fusion.1
  126.0 0.8 copy.36
  126.8 0.0 copy-done.4
  126.8 1.2 multiply_reduce_fusion
  128.1 0.6 pad.4.rate_ref
  128.7 0.7 copy.38
  129.4 56.6 %weight_gradient.1 = (f32[512,256]{1,0:T(8,128)}, f32[8,128]{1,0:T(8,128)}) custom-call(bf16[128,4096]{1,0:T(8,128)(2,1)} %bitcast.78, bf16[128,256]{1,0:T(8,128)(2,1)} %get-tuple-element.15.g_ref, f32[8,128]{1,0:T(8,128)} %pad.4.rate_ref), custom_call_target="tpu_custom_call" | custom-call | tf_op jit(solution)/shard_map/weight_gradient/pallas_call | solution.py:440
  185.9 0.0 copy-start.2
  185.9 1.2 slice_bitcast_fusion
  187.2 0.0 copy-done.1
  187.2 1.0 copy.43
  188.2 0.0 copy-done.2
  188.2 0.8 copy.44
  (5 shorter events, 0.1 us)
Async XLA Ops:
  0.6 3.1 %copy-start = (bf16[4096,256]{1,0:T(8,128)(2,1)S(1)}, bf16[4096,256]{1,0:T(8,128)(2,1)}, u32[]{:S(2)}) copy-start(bf16[4096,256]{1,0:T(8,128)(2,1)} %param.7) | copy-start | bytes 6291460
  0.6 5.4 %copy-start.3 = (f32[1,128,64]{1,2,0:T(8,128)S(1)}, f32[1,128,64]{1,2,0:T(8,128)}, u32[]{:S(2)}) copy-start(f32[1,128,64]{1,2,0:T(8,128)} %param.9) | copy-start | bytes 98308
  8.1 118.7 %copy-start.4 = (f32[64]{0:T(128)S(1)}, f32[64]{0:T(128)}, u32[]{:S(2)}) copy-start(f32[64]{0:T(128)} %param.10) | copy-start | bytes 772
  123.8 63.4 %copy-start.1 = (bf16[128,4096]{1,0:T(8,128)(2,1)S(1)}, bf16[128,4096]{1,0:T(8,128)(2,1)}, u32[]{:S(2)}) copy-start(bf16[128,4096]{1,0:T(8,128)(2,1)} %get-tuple-element.11) | copy-start | bytes 3145732
  185.9 2.2 %copy-start.2 = (f32[512,256]{1,0:T(8,128)S(1)}, f32[512,256]{1,0:T(8,128)}, u32[]{:S(2)}) copy-start(f32[512,256]{1,0:T(8,128)} %get-tuple-element.46) | copy-start | bytes 1572868

commit v5 on v4

--- a/solution.py
+++ b/solution.py
@@ -323,11 +323,8 @@
     for c in range(chunks):
         copy(c, 0).start()
     rate_copy(0).start()
-    for turn in range(chunks + count):
+    for s in range(count):
         for c in range(chunks):
-            s = turn - c
-            if not 0 <= s < count:
-                continue
             copy(c, s).wait_recv()
             keep, give, size = starts[c % 2][s]
             value = acc[c, pl.ds(keep, size)] + got[c, pl.ds(offsets[s], size)]
@@ -338,11 +335,10 @@
                 ring[0, c] = value[0]
                 for k in range(1, m):
                     out_copy(c, k).start()
-        if turn < count:
-            rate_copy(turn).wait_recv()
-            r_acc[turn + 1] = r_acc[turn] + r_got[turn]
-            if turn + 1 < count:
-                rate_copy(turn + 1).start()
+        rate_copy(s).wait_recv()
+        r_acc[s + 1] = r_acc[s] + r_got[s]
+        if s + 1 < count:
+            rate_copy(s + 1).start()
     rate_out[...] = r_acc[count]
     for c in range(chunks):
         for k in range(m):
@@ -433,7 +429,7 @@
     members = lax.axis_size("dp")
     blocks = count * members
     piece = tokens.shape[1] // blocks
-    chunks = max(1, min(8, piece // 8))
+    chunks = max(1, min(4, piece // 8))
     rows = piece // chunks
     levels = blocks.bit_length() - 1
     rate_rows = jnp.pad(grad_rate.reshape(1, heads), ((0, 7), (0, 128 - heads)))

time: 189 us -> 171 us (0.905)
  Pallas kernels: 172 us -> 154 us
    pallas_call x1, Pallas kernels: 56.6 us -> 38 us  [shards(): pl.pallas_call(functools.partial(weight_kernel, count, members), in_specs...]
where the time goes in v5:
time: 171 us; the launch traced here: 170 us
  Pallas kernels  154 us (90%)
  local copies, waits for them, and re-layouts  9.86 us (6%)
  matrix products  4 us (2%)
  other arithmetic  2.12 us (1%)
    pallas_call x1, Pallas kernels, shards(): pl.pallas_call(functools.partial(layer_kernel, count, size), in_specs=[vm...  116 us
    pallas_call x1, Pallas kernels, shards(): pl.pallas_call(functools.partial(weight_kernel, count, members), in_specs...  38 us

profile of v5, /device:TPU:0, one launch (start us, length us, event | category | flops | bytes accessed | tf_op | source)
XLA Modules:
  0.0 170.4 jit_solution(12180856528216096578)
XLA Ops:
  0.6 0.0 copy-start
  0.6 0.0 copy-start.3
  0.7 0.8 neg.27
  1.5 0.8 copy.31
  2.4 0.2 reduce_window_sum.11
  2.6 0.1 broadcast_in_dim.12
  2.7 0.1 sub.17
  2.7 0.1 broadcast_in_dim.13
  2.8 0.1 broadcast_in_dim.14
  2.9 0.1 copy.32
  3.0 0.7 copy.33
  3.7 0.0 copy-done
  3.7 1.7 convolution_convert_fusion
  5.4 0.6 fusion.20
  6.0 0.0 copy-done.3
  6.0 0.1 exponential_bitcast_fusion.1
  6.1 0.7 broadcast_in_dim.30.d_ref
  6.8 1.3 copy.34.col_ref
  8.1 0.0 copy-start.4
  8.1 115.7 %layer_gradients.1 = (bf16[128,4096]{1,0:T(8,128)(2,1)}, f32[16,4,128]{2,1,0:T(4,128)}, f32[128,192]{1,0:T(8,128)}, f32[16,1,256]{2,1,0:T(1,128)}, bf16[128,256]{1,0:T(8,128)(2,1)}) custom-call(bf16[128,128]{1,0:T(8,128)(2,1)} %get-tuple-element.35.b_ref, bf16[128,128]{1,0:T(8,128)(2,1)} %get-tuple-element.34.c_ref, bf16[128,4096]{1,0:T(8,128)(2,1)} %bitcast.79, ...), custom_call_target="tpu_custom_call" | custom-call | tf_op jit(solution)/shard_map/layer_gradients/pallas_call | solution.py:391
  123.8 0.0 copy-start.1
  123.8 0.8 reduce.2
  124.6 0.1 reshape.53
  124.7 0.1 reduce_sum.20
  124.8 1.1 convolution_add_fusion.1
  126.0 0.8 copy.36
  126.8 0.0 copy-done.4
  126.8 1.2 multiply_reduce_fusion
  128.1 0.6 pad.4.rate_ref
  128.7 0.7 copy.38
  129.4 38.0 %weight_gradient.1 = (f32[512,256]{1,0:T(8,128)}, f32[8,128]{1,0:T(8,128)}) custom-call(bf16[128,4096]{1,0:T(8,128)(2,1)} %bitcast.78, bf16[128,256]{1,0:T(8,128)(2,1)} %get-tuple-element.15.g_ref, f32[8,128]{1,0:T(8,128)} %pad.4.rate_ref), custom_call_target="tpu_custom_call" | custom-call | tf_op jit(solution)/shard_map/weight_gradient/pallas_call | solution.py:436
  167.4 0.0 copy-start.2
  167.4 1.2 slice_bitcast_fusion
  168.6 0.0 copy-done.1
  168.7 1.0 copy.43
  169.6 0.0 copy-done.2
  169.6 0.8 copy.44
  (5 shorter events, 0.1 us)
Async XLA Ops:
  0.6 3.1 %copy-start = (bf16[4096,256]{1,0:T(8,128)(2,1)S(1)}, bf16[4096,256]{1,0:T(8,128)(2,1)}, u32[]{:S(2)}) copy-start(bf16[4096,256]{1,0:T(8,128)(2,1)} %param.7) | copy-start | bytes 6291460
  0.6 5.4 %copy-start.3 = (f32[1,128,64]{1,2,0:T(8,128)S(1)}, f32[1,128,64]{1,2,0:T(8,128)}, u32[]{:S(2)}) copy-start(f32[1,128,64]{1,2,0:T(8,128)} %param.9) | copy-start | bytes 98308
  8.1 118.7 %copy-start.4 = (f32[64]{0:T(128)S(1)}, f32[64]{0:T(128)}, u32[]{:S(2)}) copy-start(f32[64]{0:T(128)} %param.10) | copy-start | bytes 772
  123.8 44.9 %copy-start.1 = (bf16[128,4096]{1,0:T(8,128)(2,1)S(1)}, bf16[128,4096]{1,0:T(8,128)(2,1)}, u32[]{:S(2)}) copy-start(bf16[128,4096]{1,0:T(8,128)(2,1)} %get-tuple-element.11) | copy-start | bytes 3145732
  167.4 2.2 %copy-start.2 = (f32[512,256]{1,0:T(8,128)S(1)}, f32[512,256]{1,0:T(8,128)}, u32[]{:S(2)}) copy-start(f32[512,256]{1,0:T(8,128)} %get-tuple-element.46) | copy-start | bytes 1572868
